TPU v7x, 256 devices: a whole 4x4x8 slice. The times are simulated.
256 devices in a mesh: dp: 64 (over z, y, x_hi), seq: 4 (over x_lo, core).
Axes of the slice: x: 4 (x_hi: 2, x_lo: 2; x = x_hi * 2 + x_lo), y: 4, z: 8, core: 2. Of those that a mesh axis runs over, the one named last changes fastest.
Arguments:
- queries: bfloat16 [32768, 2560], P(('dp', 'seq')), may hold values from -400 to 400
- key_states: bfloat16 [32768, 2560], P(('dp', 'seq')), may hold values from -400 to 400
- value_states: bfloat16 [32768, 2560], P(('dp', 'seq')), may hold values from -6 to 6
- query_tangent: bfloat16 [32768, 2560], P(('dp', 'seq')), may hold values from -6 to 6
- key_tangent: bfloat16 [32768, 2560], P(('dp', 'seq')), may hold values from -6 to 6
- value_tangent: bfloat16 [32768, 2560], P(('dp', 'seq')), may hold values from -6 to 6
- query_gain: float32 [2560], replicated, may hold values from 0.25 to 1.75
- key_gain: float32 [2560], replicated, may hold values from 0.25 to 1.75
- out_weight: bfloat16 [2560, 5120], P('seq', 'dp'), may hold values from -0.125 to 0.125
Outputs:
- projected: bfloat16 [32768, 5120], P(('dp', 'seq'))
- projected_tangent: bfloat16 [32768, 5120], P(('dp', 'seq'))
All inputs are finite; a program needn't handle non-finite values.
Results may differ from a plain program's by a relative error of at most 0.012.
The roundings to bfloat16 on the way count: a program that leaves them out, or rounds other values in their place, can miss the bound.
Values may be sent and summed in bfloat16 or wider, within the bound.
A program may use at most 128 MiB of HBM per device.

v0:
```python
import jax
import jax.numpy as jnp
from jax import lax
from jax.sharding import PartitionSpec as P

HEADS = 20
HDIM = 128


def rms_tangent(primal, tangent, gain):
    primal_f = primal.astype(jnp.float32)
    tangent_f = tangent.astype(jnp.float32)
    inverse = lax.rsqrt(jnp.mean(primal_f * primal_f, axis=-1, keepdims=True) + 1e-06)
    across = jnp.mean(primal_f * tangent_f, axis=-1, keepdims=True)
    normed = (primal_f * inverse * gain).astype(jnp.bfloat16)
    normed_tangent = (gain * (tangent_f * inverse - primal_f * inverse**3 * across)).astype(
        jnp.bfloat16
    )
    return (normed, normed_tangent)


def attend(query_normed, query_dual, key_normed, key_dual, value_plain, value_dual):
    factor = HDIM ** (-0.5)
    scores = (
        jnp.einsum("qhd,khd->hqk", query_normed, key_normed, preferred_element_type=jnp.float32)
        * factor
    )
    dual_scores = (
        jnp.einsum("qhd,khd->hqk", query_dual, key_normed, preferred_element_type=jnp.float32)
        + jnp.einsum("qhd,khd->hqk", query_normed, key_dual, preferred_element_type=jnp.float32)
    ) * factor
    peak = jnp.max(scores, axis=-1, keepdims=True)
    raised = jnp.exp(scores - peak)
    probs = raised / jnp.sum(raised, axis=-1, keepdims=True)
    spread = probs * (dual_scores - jnp.sum(probs * dual_scores, axis=-1, keepdims=True))
    probs_low = probs.astype(jnp.bfloat16)
    spread_low = spread.astype(jnp.bfloat16)
    attn = jnp.einsum(
        "hqk,khd->qhd", probs_low, value_plain, preferred_element_type=jnp.float32
    ).astype(jnp.bfloat16)
    dual_attn = (
        jnp.einsum("hqk,khd->qhd", probs_low, value_dual, preferred_element_type=jnp.float32)
        + jnp.einsum("hqk,khd->qhd", spread_low, value_plain, preferred_element_type=jnp.float32)
    ).astype(jnp.bfloat16)
    return (attn, dual_attn)


def body(
    queries,
    key_states,
    value_states,
    query_tangent,
    key_tangent,
    value_tangent,
    query_gain,
    key_gain,
    out_weight,
):
    rows_here = queries.shape[0]
    query_normed, query_dual = rms_tangent(queries, query_tangent, query_gain)
    key_normed, key_dual = rms_tangent(key_states, key_tangent, key_gain)
    by_head = (
        lax.all_to_all(
            query_normed.reshape(rows_here, HEADS, HDIM),
            "seq",
            split_axis=1,
            concat_axis=0,
            tiled=True,
        ),
        lax.all_to_all(
            query_dual.reshape(rows_here, HEADS, HDIM),
            "seq",
            split_axis=1,
            concat_axis=0,
            tiled=True,
        ),
        lax.all_to_all(
            key_normed.reshape(rows_here, HEADS, HDIM),
            "seq",
            split_axis=1,
            concat_axis=0,
            tiled=True,
        ),
        lax.all_to_all(
            key_dual.reshape(rows_here, HEADS, HDIM), "seq", split_axis=1, concat_axis=0, tiled=True
        ),
        lax.all_to_all(
            value_states.reshape(rows_here, HEADS, HDIM),
            "seq",
            split_axis=1,
            concat_axis=0,
            tiled=True,
        ),
        lax.all_to_all(
            value_tangent.reshape(rows_here, HEADS, HDIM),
            "seq",
            split_axis=1,
            concat_axis=0,
            tiled=True,
        ),
    )
    attn, dual_attn = attend(by_head[0], by_head[1], by_head[2], by_head[3], by_head[4], by_head[5])
    width_all = HEADS * HDIM
    back_plain, back_dual = (
        lax.all_to_all(attn, "seq", split_axis=0, concat_axis=1, tiled=True),
        lax.all_to_all(dual_attn, "seq", split_axis=0, concat_axis=1, tiled=True),
    )
    stacked = jnp.concatenate(
        [back_plain.reshape(rows_here, width_all), back_dual.reshape(rows_here, width_all)], axis=0
    )
    full_rows = lax.all_gather(out_weight, "seq", axis=0, tiled=True)
    result = jnp.dot(
        stacked,
        lax.all_gather(full_rows, "dp", axis=1, tiled=True),
        preferred_element_type=jnp.float32,
    ).astype(jnp.bfloat16)
    return (result[:rows_here], result[rows_here:])


def solution(mesh):
    return jax.shard_map(
        body,
        mesh=mesh,
        in_specs=(
            P(("dp", "seq"), None),
            P(("dp", "seq"), None),
            P(("dp", "seq"), None),
            P(("dp", "seq"), None),
            P(("dp", "seq"), None),
            P(("dp", "seq"), None),
            P(),
            P(),
            P("seq", "dp"),
        ),
        out_specs=(P(("dp", "seq"), None), P(("dp", "seq"), None)),
        check_vma=False,
    )
```

profile of v0, /device:TPU:1, one launch (start us, length us, event | category | flops | bytes accessed | tf_op | source)
XLA Modules:
  0.0 333.7 jit_solution(1563490094878376542)
XLA Ops:
  7.2 10.0 %all_gather.6 = bf16[2560,80]{0,1:T(8,128)(2,1)} all-gather(bf16[640,80]{0,1:T(8,128)(2,1)} %param.17), channel_id=1, replica_groups=mesh['dp'=64,'seq'=4] {'seq'}, dimensions={0}, use_global_device_ids=true | all-gather | bytes 512000 | tf_op jit(solution)/shard_map/all_gather | solution.py:111
  21.1 3.7 %all-to-all-start.1 = ((bf16[128,20,128]{0,2,1:T(8,128)(2,1)}), bf16[128,20,128]{0,2,1:T(8,128)(2,1)S(1)}, u32[]{:S(2)}, u32[]{:S(2)}) async-start(bf16[128,20,128]{0,2,1:T(8,128)(2,1)} %bitcast.5), calls=%async_computation.1 | async-start | bytes 1310720 | tf_op jit(solution)/shard_map/all_to_all | solution.py:77
  27.3 6.8 %all-to-all-done.1 = bf16[128,20,128]{0,2,1:T(8,128)(2,1)S(1)} async-done(((bf16[128,20,128]{0,2,1:T(8,128)(2,1)}), bf16[128,20,128]{0,2,1:T(8,128)(2,1)S(1)}, u32[]{:S(2)}, u32[]{:S(2)}) %all-to-all-start.1) | async-done | bytes 655392 | tf_op jit(solution)/shard_map/all_to_all | solution.py:77
  34.1 4.4 %all-to-all-start = ((bf16[128,20,128]{0,2,1:T(8,128)(2,1)}), bf16[128,20,128]{0,2,1:T(8,128)(2,1)S(1)}, u32[]{:S(2)}, u32[]{:S(2)}) async-start(bf16[128,20,128]{0,2,1:T(8,128)(2,1)} %bitcast.68), calls=%async_computation | async-start | bytes 1310720 | tf_op jit(solution)/shard_map/all_to_all | solution.py:63
  39.9 7.9 %all-to-all-done = bf16[128,20,128]{0,2,1:T(8,128)(2,1)S(1)} async-done(((bf16[128,20,128]{0,2,1:T(8,128)(2,1)}), bf16[128,20,128]{0,2,1:T(8,128)(2,1)S(1)}, u32[]{:S(2)}, u32[]{:S(2)}) %all-to-all-start) | async-done | bytes 655392 | tf_op jit(solution)/shard_map/all_to_all | solution.py:63
  47.9 13.4 %all_to_all.138 = bf16[128,20,128]{0,2,1:T(8,128)(2,1)} all-to-all(bf16[128,20,128]{0,2,1:T(8,128)(2,1)S(1)} %bitcast.65), channel_id=1, replica_groups=mesh['dp'=64,'seq'=4] {'seq'}, dimensions={1} | all-to-all | bytes 1310720 | tf_op jit(solution)/shard_map/all_to_all | solution.py:87
  61.3 13.1 %all_to_all.139 = bf16[128,20,128]{0,2,1:T(8,128)(2,1)S(1)} all-to-all(bf16[128,20,128]{0,2,1:T(8,128)(2,1)S(1)} %bitcast.67), channel_id=1, replica_groups=mesh['dp'=64,'seq'=4] {'seq'}, dimensions={1} | all-to-all | bytes 1310720 | tf_op jit(solution)/shard_map/all_to_all | solution.py:70
  74.4 4.8 %all-to-all-start.6 = ((bf16[128,20,128]{0,2,1:T(8,128)(2,1)}), bf16[128,20,128]{0,2,1:T(8,128)(2,1)S(1)}, u32[]{:S(2)}, u32[]{:S(2)}) async-start(bf16[128,20,128]{0,2,1:T(8,128)(2,1)} %bitcast.66), calls=%async_computation.6 | async-start | bytes 1310720 | tf_op jit(solution)/shard_map/all_to_all | solution.py:84
  79.2 2.2 copy.73
  82.0 1.6 copy.68
  83.7 4.1 %fusion.40 = (f32[5,512]{1,0:T(8,128)S(1)}, f32[5,512,512]{1,2,0:T(8,128)}) fusion(bf16[512,5,128]{2,0,1:T(8,128)(2,1)S(1)} %bitcast.71, bf16[512,5,128]{2,0,1:T(8,128)(2,1)S(1)} %bitcast.56), kind=kOutput, calls=%fused_computation.59 | convolution fusion | flops 339476992 | bytes 6563840 | tf_op jit(solution)/shard_map/sub | solution.py:33
  87.8 8.3 %all-to-all-done.6 = bf16[128,20,128]{0,2,1:T(8,128)(2,1)S(1)} async-done(((bf16[128,20,128]{0,2,1:T(8,128)(2,1)}), bf16[128,20,128]{0,2,1:T(8,128)(2,1)S(1)}, u32[]{:S(2)}, u32[]{:S(2)}) %all-to-all-start.6) | async-done | bytes 655392 | tf_op jit(solution)/shard_map/all_to_all | solution.py:84
  96.1 4.2 %all-to-all-start.4 = ((bf16[128,20,128]{0,2,1:T(8,128)(2,1)}), bf16[128,20,128]{0,2,1:T(8,128)(2,1)S(1)}, u32[]{:S(2)}, u32[]{:S(2)}) async-start(bf16[128,20,128]{0,2,1:T(8,128)(2,1)} %bitcast.20), calls=%async_computation.4 | async-start | bytes 1310720 | tf_op jit(solution)/shard_map/all_to_all | solution.py:94
  100.3 3.5 %fusion.32 = bf16[512,5,128]{2,0,1:T(8,128)(2,1)S(1)} fusion(bf16[512,5,128]{2,0,1:T(8,128)(2,1)S(1)} %bitcast.69, f32[5,512,512]{1,2,0:T(8,128)} %get-tuple-element.17, f32[5,512]{1,0:T(8,128)S(1)} %get-tuple-element.16), kind=kOutput, calls=%fused_computation.48 | convolution fusion | flops 338493440 | bytes 6563840 | tf_op jit(solution)/shard_map/hqk,khd->qhd/dot_general | solution.py:38
  106.7 4.9 %all-to-all-done.4 = bf16[128,20,128]{0,2,1:T(8,128)(2,1)S(1)} async-done(((bf16[128,20,128]{0,2,1:T(8,128)(2,1)}), bf16[128,20,128]{0,2,1:T(8,128)(2,1)S(1)}, u32[]{:S(2)}, u32[]{:S(2)}) %all-to-all-start.4) | async-done | bytes 655392 | tf_op jit(solution)/shard_map/all_to_all | solution.py:94
  111.6 3.9 %all-to-all-start.3 = ((bf16[512,5,128]{2,1,0:T(8,128)(2,1)}), bf16[512,5,128]{2,1,0:T(8,128)(2,1)S(1)}, u32[]{:S(2)}, u32[]{:S(2)}) async-start(bf16[512,5,128]{2,1,0:T(8,128)(2,1)} %copy.70), calls=%async_computation.3 | async-start | bytes 2097152 | tf_op jit(solution)/shard_map/all_to_all | solution.py:105
  117.7 1.7 copy-done.11
  120.7 1.8 multiply_reduce_fusion
  125.3 3.8 %all-to-all-done.3 = bf16[512,5,128]{2,1,0:T(8,128)(2,1)S(1)} async-done(((bf16[512,5,128]{2,1,0:T(8,128)(2,1)}), bf16[512,5,128]{2,1,0:T(8,128)(2,1)S(1)}, u32[]{:S(2)}, u32[]{:S(2)}) %all-to-all-start.3) | async-done | bytes 655392 | tf_op jit(solution)/shard_map/all_to_all | solution.py:105
  129.1 4.4 %all-to-all-start.7 = ((bf16[512,5,128]{2,1,0:T(8,128)(2,1)}), bf16[512,5,128]{2,1,0:T(8,128)(2,1)S(1)}, u32[]{:S(2)}, u32[]{:S(2)}) async-start(bf16[512,5,128]{2,1,0:T(8,128)(2,1)} %copy.84), calls=%async_computation.7 | async-start | bytes 2097152 | tf_op jit(solution)/shard_map/all_to_all | solution.py:106
  134.1 12.8 %all-to-all-done.7 = bf16[512,5,128]{2,1,0:T(8,128)(2,1)S(1)} async-done(((bf16[512,5,128]{2,1,0:T(8,128)(2,1)}), bf16[512,5,128]{2,1,0:T(8,128)(2,1)S(1)}, u32[]{:S(2)}, u32[]{:S(2)}) %all-to-all-start.7) | async-done | bytes 655392 | tf_op jit(solution)/shard_map/all_to_all | solution.py:106
  148.2 164.7 %all-gather.2.cloned.1.call-done = bf16[2560,5120]{0,1:T(8,128)(2,1)} async-done(((bf16[2560,80]{0,1:T(8,128)(2,1)}), bf16[2560,5120]{0,1:T(8,128)(2,1)}) %all-gather.2.cloned.1.call-update) | async-done | bytes 26214416 | tf_op jit(solution)/shard_map/all_gather | solution.py:114
  312.9 12.3 %convolution_convert_fusion = bf16[256,5120]{1,0:T(8,128)(2,1)S(1)} fusion(bf16[2560,5120]{0,1:T(8,128)(2,1)} %all-gather.2.cloned.1.call-done, bf16[128,2560]{0,1:T(8,128)(2,1)} %bitcast.75, bf16[128,2560]{0,1:T(8,128)(2,1)S(1)} %bitcast.74), kind=kOutput, calls=%fused_computation.1 | convolution fusion | flops 6714818560 | bytes 30146560 | tf_op jit(solution)/shard_map/dot_general | solution.py:112
  325.2 1.7 fusion.39
  (48 shorter events, 19.3 us)
Async XLA Ops:
  7.2 11.5 %copy-start = (bf16[128,2560]{1,0:T(8,128)(2,1)S(1)}, bf16[128,2560]{1,0:T(8,128)(2,1)}, u32[]{:S(2)}) copy-start(bf16[128,2560]{1,0:T(8,128)(2,1)} %param.13) | copy-start | bytes 1966084
  7.2 12.3 %copy-start.9 = (f32[2560]{0:T(1024)S(1)}, f32[2560]{0:T(1024)}, u32[]{:S(2)}) copy-start(f32[2560]{0:T(1024)} %param.16) | copy-start | bytes 30724
  7.2 305.7 %all-gather.2.cloned.1.call-start = ((), (), s32[]{:S(2)}) async-start(), calls=%async_computation.8 | async-start | bytes 26624000 | tf_op jit(solution)/shard_map/all_gather | solution.py:114
  19.0 5.8 %copy-start.1 = (bf16[128,2560]{1,0:T(8,128)(2,1)S(1)}, bf16[128,2560]{1,0:T(8,128)(2,1)}, u32[]{:S(2)}) copy-start(bf16[128,2560]{1,0:T(8,128)(2,1)} %param.9) | copy-start | bytes 1966084
  19.4 5.7 %copy-start.2 = (bf16[128,2560]{1,0:T(8,128)(2,1)S(1)}, bf16[128,2560]{1,0:T(8,128)(2,1)}, u32[]{:S(2)}) copy-start(bf16[128,2560]{1,0:T(8,128)(2,1)} %param.12) | copy-start | bytes 1966084
  21.1 4.8 %copy-start.10 = (f32[2560]{0:T(1024)S(1)}, f32[2560]{0:T(1024)}, u32[]{:S(2)}) copy-start(f32[2560]{0:T(1024)} %param.15) | copy-start | bytes 30724
  21.1 13.0 %all-to-all-start.1 = ((bf16[128,20,128]{0,2,1:T(8,128)(2,1)}), bf16[128,20,128]{0,2,1:T(8,128)(2,1)S(1)}, u32[]{:S(2)}, u32[]{:S(2)}) async-start(bf16[128,20,128]{0,2,1:T(8,128)(2,1)} %bitcast.5), calls=%async_computation.1 | async-start | bytes 1310720 | tf_op jit(solution)/shard_map/all_to_all | solution.py:77
  34.1 13.8 %all-to-all-start = ((bf16[128,20,128]{0,2,1:T(8,128)(2,1)}), bf16[128,20,128]{0,2,1:T(8,128)(2,1)S(1)}, u32[]{:S(2)}, u32[]{:S(2)}) async-start(bf16[128,20,128]{0,2,1:T(8,128)(2,1)} %bitcast.68), calls=%async_computation | async-start | bytes 1310720 | tf_op jit(solution)/shard_map/all_to_all | solution.py:63
  74.4 21.7 %all-to-all-start.6 = ((bf16[128,20,128]{0,2,1:T(8,128)(2,1)}), bf16[128,20,128]{0,2,1:T(8,128)(2,1)S(1)}, u32[]{:S(2)}, u32[]{:S(2)}) async-start(bf16[128,20,128]{0,2,1:T(8,128)(2,1)} %bitcast.66), calls=%async_computation.6 | async-start | bytes 1310720 | tf_op jit(solution)/shard_map/all_to_all | solution.py:84
  82.0 5.8 %copy-start.5 = (bf16[4,128,5,128]{3,1,0,2:T(8,128)(2,1)}, bf16[4,128,5,128]{3,1,0,2:T(8,128)(2,1)S(1)}, u32[]{:S(2)}) copy-start(bf16[4,128,5,128]{3,1,0,2:T(8,128)(2,1)S(1)} %copy.62) | copy-start | bytes 1966084
  83.7 16.6 %copy-start.3 = (bf16[4,128,5,128]{3,1,0,2:T(8,128)(2,1)}, bf16[4,128,5,128]{3,1,0,2:T(8,128)(2,1)S(1)}, u32[]{:S(2)}) copy-start(bf16[4,128,5,128]{3,1,0,2:T(8,128)(2,1)S(1)} %copy.68) | copy-start | bytes 1966084
  96.1 15.5 %all-to-all-start.4 = ((bf16[128,20,128]{0,2,1:T(8,128)(2,1)}), bf16[128,20,128]{0,2,1:T(8,128)(2,1)S(1)}, u32[]{:S(2)}, u32[]{:S(2)}) async-start(bf16[128,20,128]{0,2,1:T(8,128)(2,1)} %bitcast.20), calls=%async_computation.4 | async-start | bytes 1310720 | tf_op jit(solution)/shard_map/all_to_all | solution.py:94
  111.6 17.5 %all-to-all-start.3 = ((bf16[512,5,128]{2,1,0:T(8,128)(2,1)}), bf16[512,5,128]{2,1,0:T(8,128)(2,1)S(1)}, u32[]{:S(2)}, u32[]{:S(2)}) async-start(bf16[512,5,128]{2,1,0:T(8,128)(2,1)} %copy.70), calls=%async_computation.3 | async-start | bytes 2097152 | tf_op jit(solution)/shard_map/all_to_all | solution.py:105
  116.6 1.1 copy-start.8
  116.6 2.8 copy-start.11
  119.4 1.1 copy-start.6
  119.4 1.3 copy-start.7
  120.7 1.8 copy-start.4
  129.1 17.8 %all-to-all-start.7 = ((bf16[512,5,128]{2,1,0:T(8,128)(2,1)}), bf16[512,5,128]{2,1,0:T(8,128)(2,1)S(1)}, u32[]{:S(2)}, u32[]{:S(2)}) async-start(bf16[512,5,128]{2,1,0:T(8,128)(2,1)} %copy.84), calls=%async_computation.7 | async-start | bytes 2097152 | tf_op jit(solution)/shard_map/all_to_all | solution.py:106
Sparse Core Ops, SparseCore 0:
  17.4 295.4 all-gather.1
where the time goes:
time: 335 us; the launch traced here: 334 us
  waiting for transfers between devices  209 us (62%)
  blocking collectives  36.5 us (11%)
  starting transfers between devices  25.5 us (8%)
  matrix products  24.9 us (7%)
  local copies, waits for them, and re-layouts  19.4 us (6%)
  between operations  14.2 us (4%)
  other arithmetic  3.83 us (1%)
    all_gather x1, waiting for transfers between devices, body(): lax.all_gather(full_rows, 'dp', axis=1, tiled=True)  165 us
    all_to_all x1, blocking collectives, body(): lax.all_to_all(value_states.reshape(rows_here, HEADS, HDIM), 'seq', split...  13.4 us
    all_to_all x1, blocking collectives, body(): lax.all_to_all(query_dual.reshape(rows_here, HEADS, HDIM), 'seq', split_a...  13.1 us
    all_to_all x1, waiting for transfers between devices, body(): lax.all_to_all(dual_attn, 'seq', split_axis=0, concat_axis=1, tiled=True)  12.8 us
    dot_general x1, matrix products, body(): jnp.dot(stacked, lax.all_gather(full_rows, 'dp', axis=1, tiled=True), pre...  12.3 us
    all_gather x1, blocking collectives, body(): full_rows = lax.all_gather(out_weight, 'seq', axis=0, tiled=True)  10 us
    all_to_all x1, waiting for transfers between devices, body(): lax.all_to_all(key_dual.reshape(rows_here, HEADS, HDIM), 'seq', split_axi...  8.3 us
    unnamed x30, local copies, waits for them, and re-layouts  8.14 us
  transfers between devices with their start and end apart: 7, of which 7 were waited for; matrix products, arithmetic and copies ran while one was open for 10% of the time, Pallas kernels for 0%

commit v1 on v0

v1 whole, which is shorter than its diff:
```python
import jax
import jax.numpy as jnp
from jax import lax
from jax.experimental import pallas as pl
from jax.experimental.pallas import tpu as pltpu
from jax.sharding import PartitionSpec as P

HDIM = 128
NZ, NY = 8, 4
ROWS = 128
BLK = 640
UNIT = 80
PLANE = 640
EPS = 1e-06
MESH = pl.DeviceIdType.MESH
BF16 = jnp.bfloat16
F32 = jnp.float32


def rms_tangent(primal_ref, tangent_ref, gain_ref, normed_ref, dual_ref):
    width = primal_ref.shape[1]
    for row in range(0, ROWS, 32):
        rows = pl.ds(row, 32)
        primal = primal_ref[rows, :].astype(F32)
        tangent = tangent_ref[rows, :].astype(F32)
        inverse = lax.rsqrt(jnp.sum(primal * primal, axis=-1, keepdims=True) * (1.0 / width) + EPS)
        across = jnp.sum(primal * tangent, axis=-1, keepdims=True) * (1.0 / width)
        pull = inverse * inverse * inverse * across
        gain = gain_ref[...]
        normed = (primal * inverse * gain).astype(BF16)
        dual = (gain * (tangent * inverse - primal * pull)).astype(BF16)
        for block in range(4):
            normed_ref[block, rows, :] = normed[:, block * BLK : (block + 1) * BLK]
            dual_ref[block, rows, :] = dual[:, block * BLK : (block + 1) * BLK]


def kernel(
    q_in,
    dq_in,
    k_in,
    dk_in,
    v_in,
    dv_in,
    q_gain,
    k_gain,
    w_in,
    out,
    dual_out,
    w_all,
    qn,
    dqn,
    kn,
    dkn,
    q_all,
    dq_all,
    k_all,
    dk_all,
    v_all,
    dv_all,
    attn,
    acc,
    give,
    got,
    done,
    w_recv,
    w_send,
    first_sem,
    kv_recv,
    kv_send,
    q_recv,
    q_send,
    own_sem,
    part_recv,
    part_send,
    out_sem,
):
    dp = lax.axis_index("dp")
    seq = lax.axis_index("seq")
    z, y, hi = dp // 8, lax.rem(dp // 2, 4), lax.rem(dp, 2)
    lo, core = seq // 2, lax.rem(seq, 2)
    way = 1 - 2 * core

    def unit(zz, yy, hh):
        return zz * 8 + yy * 2 + hh

    def z_at(off):
        return lax.rem(z + off * way + NZ, NZ)

    def y_at(off):
        return lax.rem(y + off * way + NY, NY)

    side = {
        "zf": (unit(z_at(1), y, hi), seq),
        "zb": (unit(z_at(-1), y, hi), seq),
        "yf": (unit(z, y_at(1), hi), seq),
        "yb": (unit(z, y_at(-1), hi), seq),
        "hi": (unit(z, y, 1 - hi), (1 - lo) * 2 + core),
        "lo": (dp, (1 - lo) * 2 + core),
        "cross": (dp, (1 - lo) * 2 + 1 - core),
        "mate": (dp, lo * 2 + 1 - core),
    }

    barrier = pltpu.get_barrier_semaphore()
    for target in side.values():
        pl.semaphore_signal(barrier, inc=1, device_id=target, device_id_type=MESH)
    pl.semaphore_wait(barrier, len(side))

    def remote(src, dst, send_sem, recv_sem, to):
        return pltpu.make_async_remote_copy(
            src_ref=src,
            dst_ref=dst,
            send_sem=send_sem,
            recv_sem=recv_sem,
            device_id=side[to],
            device_id_type=MESH,
        )

    own_w = pltpu.make_async_copy(w_in, w_all.at[lo, dp], first_sem.at[0])
    own_w.start()
    lo_w = remote(w_in, w_all.at[lo, dp], first_sem.at[1], first_sem.at[2], "lo")
    lo_w.start()

    def mine(group):
        return core + 2 * group

    def theirs(group):
        return 1 - core + 2 * group

    def columns(block):
        return pl.ds(pl.multiple_of(block * BLK, 128), BLK)

    def kv_source(tensor, block):
        if tensor == 0:
            return kn.at[block]
        if tensor == 1:
            return dkn.at[block]
        return (v_in if tensor == 2 else dv_in).at[:, columns(block)]

    kv_home = (k_all, dk_all, v_all, dv_all)
    kv_to = ("mate", "lo", "cross")

    def kv_copy(group, tensor, which):
        to = kv_to[which]
        block = mine(group) if to == "lo" else theirs(group)
        return remote(
            kv_source(tensor, block),
            kv_home[tensor].at[group, pl.ds((which + 1) * ROWS, ROWS), :],
            kv_send.at[group, tensor, which],
            kv_recv.at[group, tensor, which],
            to,
        )

    def kv_own(group, tensor):
        return pltpu.make_async_copy(
            kv_source(tensor, mine(group)),
            kv_home[tensor].at[group, pl.ds(0, ROWS), :],
            own_sem.at[group, tensor],
        )

    q_from, q_home = (qn, dqn), (q_all, dq_all)

    def q_copy(group, tensor):
        return remote(
            q_from[tensor].at[theirs(group)],
            q_home[tensor].at[group, pl.ds(ROWS, ROWS), :],
            q_send.at[group, tensor],
            q_recv.at[group, tensor],
            "mate",
        )

    def q_own(group, tensor):
        return pltpu.make_async_copy(
            q_from[tensor].at[mine(group)],
            q_home[tensor].at[group, pl.ds(0, ROWS), :],
            own_sem.at[group, 4 + tensor],
        )

    def start_kv(group, tensors):
        for which in (1, 2, 0):
            for tensor in tensors:
                kv_copy(group, tensor, which).start()
        for tensor in tensors:
            kv_own(group, tensor).start()

    def start_q(group):
        for tensor in range(2):
            q_copy(group, tensor).start()
            q_own(group, tensor).start()

    def wait_group(group):
        for tensor in range(4):
            kv_own(group, tensor).wait()
            for which in range(3):
                kv_copy(group, tensor, which).wait_recv()
        for tensor in range(2):
            q_own(group, tensor).wait()
            q_copy(group, tensor).wait_recv()

    start_kv(0, (2, 3))
    rms_tangent(k_in, dk_in, k_gain, kn, dkn)

    def piece(stream, source):
        if stream == 0:
            return w_all.at[:, source, pl.ds(0, 32), :]
        return w_all.at[stream - 1, source, pl.ds(32, 48), :]

    def w_copy(stream, source, to):
        where = piece(stream, source)
        return remote(where, where, w_send.at[stream], w_recv.at[stream, source], to)

    def pass_on(stream, source, targets):
        for to in targets:
            w_copy(stream, source, to).start()

    def arrive(stream, source, targets=()):
        w_copy(stream, source, "zf").wait_recv()
        pass_on(stream, source, targets)

    y_offs = (0, 1, -1, 2)

    def src(zo, yo, flip):
        return unit(z_at(-zo), y_at(-yo), 1 - hi if flip else hi)

    def z_next(zo):
        if zo > 0:
            return ("zf",) if zo < 4 else ()
        return ("zb",) if zo > -3 else ()

    events = []

    def note(*what):
        events.append(lambda: arrive(*what))

    def ring(r):
        return (0,) if r == 0 else ((4,) if r == 4 else (r, -r))

    def s0_z(r):
        for zo in ring(r):
            note(0, src(zo, 0, False), z_next(zo) + ("yf", "yb", "hi"))

    def s0_y(r):
        for zo in ring(r):
            note(0, src(zo, 1, False), ("yf", "hi"))
            note(0, src(zo, -1, False), ("hi",))
        for zo in ring(r):
            note(0, src(zo, 2, False), ("hi",))

    def s0_end(r):
        for zo in ring(r):
            for yo in y_offs:
                note(0, src(zo, yo, True), ())

    def s1_y():
        for flip in (False, True):
            note(1, src(0, 1, flip), ("yf", "zf", "zb"))
            note(1, src(0, -1, flip), ("zf", "zb"))
        for flip in (False, True):
            note(1, src(0, 2, flip), ("zf", "zb"))

    def s1_z(r):
        for yo in y_offs:
            for flip in (False, True):
                for zo in ring(r):
                    note(1, src(zo, yo, flip), z_next(zo))

    def s2_z(r):
        for flip in (False, True):
            for zo in ring(r):
                note(2, src(zo, 0, flip), z_next(zo) + ("yf", "yb"))

    def s2_y(r):
        for zo in ring(r):
            for flip in (False, True):
                note(2, src(zo, 1, flip), ("yf",))
                note(2, src(zo, -1, flip), ())
        for zo in ring(r):
            for flip in (False, True):
                note(2, src(zo, 2, flip), ())

    own_w.wait()
    lo_w.wait_recv()
    pass_on(1, dp, ("hi",))
    pass_on(2, dp, ("hi",))
    pass_on(0, dp, ("zf", "zb", "yf", "yb", "hi"))
    pass_on(1, dp, ("yf", "yb", "zf", "zb"))
    pass_on(2, dp, ("zf", "zb", "yf", "yb"))

    rms_tangent(q_in, dq_in, q_gain, qn, dqn)
    start_kv(0, (0, 1))
    start_q(0)
    start_q(1)
    start_kv(1, (2, 3))
    start_kv(1, (0, 1))

    factor = HDIM ** (-0.5)
    nt = (((1,), (1,)), ((), ()))

    def head(group, index):
        cols = pl.ds(index * HDIM, HDIM)
        queries, dual_queries = q_all[group, :, cols], dq_all[group, :, cols]
        keys, dual_keys = k_all[group, :, cols], dk_all[group, :, cols]
        values, dual_values = v_all[group, :, cols], dv_all[group, :, cols]
        scores = lax.dot_general(queries, keys, nt, preferred_element_type=F32) * factor
        dual_scores = (
            lax.dot_general(
                jnp.concatenate([dual_queries, queries], axis=1),
                jnp.concatenate([keys, dual_keys], axis=1),
                nt,
                preferred_element_type=F32,
            )
            * factor
        )
        raised = jnp.exp(scores - jnp.max(scores, axis=-1, keepdims=True))
        probs = raised * (1.0 / jnp.sum(raised, axis=-1, keepdims=True))
        spread = probs * (dual_scores - jnp.sum(probs * dual_scores, axis=-1, keepdims=True))
        low = probs.astype(BF16)
        both = jnp.dot(
            low, jnp.concatenate([values, dual_values], axis=1), preferred_element_type=F32
        )
        dual = both[:, HDIM:] + jnp.dot(spread.astype(BF16), values, preferred_element_type=F32)
        plain = both[:, :HDIM].astype(BF16)
        dual = dual.astype(BF16)
        for owner in range(2):
            rows = slice(owner * ROWS, (owner + 1) * ROWS)
            attn[group, pl.ds(owner * 256, ROWS), cols] = plain[rows]
            attn[group, pl.ds(owner * 256 + ROWS, ROWS), cols] = dual[rows]

    plane_offs = (0, -1, 1, -2, 2, -3, 3, 4)

    def plane_of(index):
        return lax.rem(z + plane_offs[index] + NZ, NZ)

    def product(group, plane):
        first = pl.multiple_of(plane * 8, 8)
        weight = w_all[group, pl.ds(first, 8)].reshape(PLANE, BLK)
        return lax.dot_general(attn[group], weight, nt, preferred_element_type=F32)

    def half_one(index):
        acc[index] = product(0, plane_of(index))

    def part_copy(plane, index):
        return remote(
            give.at[index], got.at[plane], part_send.at[index], part_recv.at[plane], "mate"
        )

    def half_two(index):
        plane = plane_of(index)
        total = acc[index] + product(1, plane)
        acc[index, pl.ds(0, 256), :] = total[:256]
        give[index] = total[256:].astype(BF16)
        part_copy(plane, index).start()

    def out_copies(index):
        plane = plane_of(index)
        cols = pl.ds(pl.multiple_of(plane * PLANE, 128), PLANE)
        return [
            pltpu.make_async_copy(
                done.at[index, pl.ds(half * ROWS, ROWS), :],
                (out, dual_out)[half].at[:, cols],
                out_sem.at[index, half],
            )
            for half in range(2)
        ]

    def finish(index):
        plane = plane_of(index)
        part_copy(plane, index).wait_recv()
        done[index] = (acc[index, pl.ds(0, 256), :] + got[plane].astype(F32)).astype(BF16)
        for copy in out_copies(index):
            copy.start()

    def weave(tasks):
        pending, count = list(events), len(tasks)
        events.clear()
        at = 0
        for place, event in enumerate(pending):
            event()
            while at < count and (at + 1) * len(pending) <= (place + 1) * count:
                tasks[at]()
                at += 1
        for task in tasks[at:]:
            task()

    note(1, src(0, 0, True), ("yf", "yb", "zf", "zb"))
    note(2, src(0, 0, True), ("zf", "zb", "yf", "yb"))
    s0_z(1)
    s1_y()
    s0_y(0)
    s2_z(1)
    s2_y(0)
    s0_z(2)
    s0_y(1)
    s1_z(1)
    s0_end(0)
    s2_z(2)
    s2_y(1)
    s0_z(3)
    s0_y(2)
    s1_z(2)
    s0_end(1)
    s2_z(3)
    s2_y(2)
    weave([])
    wait_group(0)
    s0_z(4)
    s0_y(3)
    s1_z(3)
    s0_end(2)
    s2_z(4)
    s2_y(3)
    weave([lambda i=i: head(0, i) for i in range(5)])
    s0_y(4)
    s1_z(4)
    s0_end(3)
    s2_y(4)
    s0_end(4)
    weave([lambda i=i: half_one(i) for i in range(5)])
    wait_group(1)
    for i in range(5):
        head(1, i)
    for i in range(5, 8):
        half_one(i)
    for i in range(8):
        half_two(i)
        if i > 0:
            finish(i - 1)
    finish(7)

    lo_w.wait_send()
    for group in range(2):
        for tensor in range(4):
            for which in range(3):
                kv_copy(group, tensor, which).wait_send()
        for tensor in range(2):
            q_copy(group, tensor).wait_send()
    sent = (w_all.at[:, pl.ds(0, 63), pl.ds(0, 32), :],) + tuple(
        w_all.at[j, pl.ds(0, 63), pl.ds(32, 48), :] for j in range(2)
    )
    for stream in range(3):
        pltpu.make_async_copy(sent[stream], sent[stream], w_send.at[stream]).wait()
    for index in range(8):
        part_copy(plane_of(index), index).wait_send()
        for copy in out_copies(index):
            copy.wait()


def body(q, k, v, dq, dk, dv, q_gain, k_gain, weight):
    rows, width = q.shape
    vmem = pl.BlockSpec(memory_space=pltpu.VMEM)
    hbm = pl.BlockSpec(memory_space=pl.ANY)
    sem = pltpu.SemaphoreType.DMA
    kv = pltpu.VMEM((2, 4 * ROWS, BLK), BF16)
    qs = pltpu.VMEM((2, 2 * ROWS, BLK), BF16)
    normed = pltpu.VMEM((4, ROWS, BLK), BF16)
    shape = jax.ShapeDtypeStruct((rows, 2 * width), BF16)
    return pl.pallas_call(
        kernel,
        out_shape=(shape, shape),
        in_specs=[vmem] * 4 + [hbm] * 2 + [vmem] * 2 + [hbm],
        out_specs=(hbm, hbm),
        scratch_shapes=[
            pltpu.VMEM((2, 64, UNIT, BLK), BF16),
            normed,
            normed,
            normed,
            normed,
            qs,
            qs,
            kv,
            kv,
            kv,
            kv,
            pltpu.VMEM((2, 4 * ROWS, BLK), BF16),
            pltpu.VMEM((8, 4 * ROWS, PLANE), F32),
            pltpu.VMEM((8, 2 * ROWS, PLANE), BF16),
            pltpu.VMEM((8, 2 * ROWS, PLANE), BF16),
            pltpu.VMEM((8, 2 * ROWS, PLANE), BF16),
            sem((3, 64)),
            sem((3,)),
            sem((3,)),
            sem((2, 4, 3)),
            sem((2, 4, 3)),
            sem((2, 2)),
            sem((2, 2)),
            sem((2, 6)),
            sem((8,)),
            sem((8,)),
            sem((8, 2)),
        ],
        compiler_params=pltpu.CompilerParams(
            collective_id=0, has_side_effects=True, vmem_limit_bytes=60 * 1024 * 1024
        ),
        name="tangent_attention",
    )(q, dq, k, dk, v, dv, q_gain.reshape(1, width), k_gain.reshape(1, width), weight.T)


def solution(mesh):
    tokens = P(("dp", "seq"), None)
    return jax.shard_map(
        body,
        mesh=mesh,
        in_specs=(tokens,) * 6 + (P(), P(), P("seq", "dp")),
        out_specs=(tokens, tokens),
        check_vma=False,
    )
```

time: 335 us -> 126 us (0.38)
  waiting for transfers between devices: 209 us -> 0 us
  Pallas kernels: 0 us -> 117 us
  blocking collectives: 36.5 us -> 0 us
  starting transfers between devices: 25.5 us -> 0 us
  matrix products: 24.9 us -> 0 us
  between operations: 14.2 us -> 0.65 us
  local copies, waits for them, and re-layouts: 19.4 us -> 6.25 us
  other arithmetic: 3.83 us -> 0 us
    all_gather x1 -> x0, waiting for transfers between devices: 165 us -> none  [body(): lax.all_gather(full_rows, 'dp', axis=1, tiled=True)]
    pallas_call x0 -> x1, Pallas kernels: none -> 117 us  [body(): pl.pallas_call(kernel, out_shape=(shape, shape), in_specs=[vmem] * 4 + [h...]
    all_to_all x6 -> x0, waiting for transfers between devices: 44.6 us -> none  [the longest x1 12.8 us: body(): lax.all_to_all(dual_attn, 'seq', split_axis=0, concat_axis=1, tiled=True)]
    all_to_all x2 -> x0, blocking collectives: 26.5 us -> none  [the longest x1 13.4 us: body(): lax.all_to_all(value_states.reshape(rows_here, HEADS, HDIM), 'seq', split...]
    all_to_all x6 -> x0, starting transfers between devices: 25.4 us -> none  [the longest x1 4.79 us: body(): lax.all_to_all(key_dual.reshape(rows_here, HEADS, HDIM), 'seq', split_axi...]
    dot_general x6 -> x0, matrix products: 20.8 us -> none  [the longest x1 12.3 us: body(): jnp.dot(stacked, lax.all_gather(full_rows, 'dp', axis=1, tiled=True), pre...]
    all_gather x1 -> x0, blocking collectives: 10 us -> none  [body(): full_rows = lax.all_gather(out_weight, 'seq', axis=0, tiled=True)]
    all_to_all x8 -> x0, local copies, waits for them, and re-layouts: 6.72 us -> none  [the longest x1 1.64 us: body(): lax.all_to_all(value_states.reshape(rows_here, HEADS, HDIM), 'seq', split...]
  transfers between devices with their start and end apart: 7 -> 0, of which waited for: 7 -> 0; matrix products, arithmetic and copies ran while one was open for 10% -> 0% of each run, Pallas kernels for 0% -> 0%
where the time goes in v1:
time: 126 us; the launch traced here: 124 us
  Pallas kernels  117 us (93%)
  local copies, waits for them, and re-layouts  6.25 us (5%)
    pallas_call x1, Pallas kernels, body(): pl.pallas_call(kernel, out_shape=(shape, shape), in_specs=[vmem] * 4 + [h...  117 us
    unnamed x4, local copies, waits for them, and re-layouts  3.62 us

profile of v1, /device:TPU:1, one launch (start us, length us, event | category | flops | bytes accessed | tf_op | source)
XLA Modules:
  0.0 123.9 jit_solution(9413356062314761347)
XLA Ops:
  0.6 1.3 %reshape.10.q_gain = f32[1,2560]{1,0:T(1,128)} reshape(f32[2560]{0:T(1024)} %param.15) | data formatting | bytes 20480 | tf_op jit(solution)/shard_map/reshape | solution.py:494
  1.9 1.3 %reshape.11.k_gain = f32[1,2560]{1,0:T(1,128)} reshape(f32[2560]{0:T(1024)} %param.16) | data formatting | bytes 20480 | tf_op jit(solution)/shard_map/reshape | solution.py:494
  3.3 117.0 %tangent_attention.1 = (bf16[128,5120]{1,0:T(8,128)(2,1)}, bf16[128,5120]{1,0:T(8,128)(2,1)}) custom-call(bf16[128,2560]{1,0:T(8,128)(2,1)} %q_in.1, bf16[128,2560]{1,0:T(8,128)(2,1)} %dq_in.1, bf16[128,2560]{1,0:T(8,128)(2,1)} %k_in.1, bf16[128,2560]{1,0:T(8,128)(2,1)} %dk_in.1, bf16[128,2560]{1,0:T(8,128)(2,1)} %v_in.1, bf16[128,2560]{1,0:T(8,128)(2,1)} %dv_in.1, ...), custom_call_target="tpu_custom_call" | custom-call | tf_op jit(solution)/shard_map/tangent_attention/pallas_call | solution.py:456
  120.3 0.0 copy-start
  120.3 2.6 %copy.13 = bf16[128,5120]{1,0:T(8,128)(2,1)} copy(bf16[128,5120]{1,0:T(8,128)(2,1)} %get-tuple-element.4) | data formatting | bytes 2621440
  122.9 0.0 copy-done
  122.9 1.1 copy.14
Async XLA Ops:
  120.3 2.6 %copy-start = (bf16[128,5120]{1,0:T(8,128)(2,1)S(1)}, bf16[128,5120]{1,0:T(8,128)(2,1)}, u32[]{:S(2)}) copy-start(bf16[128,5120]{1,0:T(8,128)(2,1)} %get-tuple-element.5) | copy-start | bytes 3932164

commit v2 on v1

v2 whole, which is shorter than its diff:
```python
import jax
import jax.numpy as jnp
from jax import lax
from jax.experimental import pallas as pl
from jax.experimental.pallas import tpu as pltpu
from jax.sharding import PartitionSpec as P

HDIM = 128
NZ, NY = 8, 4
ROWS = 128
BLK = 640
UNIT = 80
PLANE = 640
EPS = 1e-06
MESH = pl.DeviceIdType.MESH
BF16 = jnp.bfloat16
F32 = jnp.float32

Z_OFFS = (0, 1, -1, 2, -2, 3, -3, 4)
Y_OFFS = (0, 1, -1, 2)
SECOND, KEY_NORM, KEYS, QUERY_NORM, QUERIES, HEAD = 200, 201, 202, 203, 204, 300
FIRST, MIDDLE, LAST, REST, WHOLE, FINISH = 400, 410, 420, 430, 440, 450
ORDER = (
    201, 202, 72, 80, 66, 68, 65, 200, 203, 204, 88, 70, 96, 69, 1, 4, 74, 67, 82, 129, 2, 132, 76,
    84, 130, 73, 81, 71, 300, 5, 8, 16, 133, 131, 6, 136, 144, 3, 134, 104, 86, 78, 112, 10, 12, 9,
    301, 77, 85, 18, 20, 17, 90, 83, 135, 140, 7, 75, 98, 138, 148, 137, 145, 146, 11, 14, 92, 302,
    100, 22, 13, 89, 97, 141, 142, 19, 79, 87, 149, 139, 147, 21, 24, 32, 150, 303, 152, 143, 160,
    15, 151, 120, 102, 23, 28, 26, 94, 101, 25, 93, 36, 99, 34, 106, 156, 114, 304, 33, 154, 91,
    164, 161, 162, 400, 29, 30, 153, 116, 401, 38, 27, 108, 113, 402, 158, 165, 105, 103, 37, 305,
    163, 157, 95, 166, 48, 35, 155, 40, 176, 31, 168, 118, 167, 39, 110, 404, 117, 52, 50, 306, 109,
    115, 49, 44, 159, 122, 177, 403, 180, 41, 107, 119, 42, 172, 169, 53, 178, 124, 181, 121, 307,
    170, 111, 51, 56, 410, 173, 54, 184, 179, 411, 45, 126, 46, 412, 125, 413, 123, 171, 43, 185,
    414, 60, 127, 182, 308, 57, 188, 174, 55, 189, 58, 186, 183, 406, 47, 175, 405, 187, 61, 309,
    62, 190, 420, 59, 421, 191, 422, 423, 450, 424, 451, 452, 63, 435, 453, 454, 436, 447, 455, 456,
    457,
)


def rms_tangent(primal_ref, tangent_ref, gain_ref, normed_ref, dual_ref):
    width = primal_ref.shape[1]
    for row in range(0, ROWS, 32):
        rows = pl.ds(row, 32)
        primal = primal_ref[rows, :].astype(F32)
        tangent = tangent_ref[rows, :].astype(F32)
        inverse = lax.rsqrt(jnp.sum(primal * primal, axis=-1, keepdims=True) * (1.0 / width) + EPS)
        across = jnp.sum(primal * tangent, axis=-1, keepdims=True) * (1.0 / width)
        pull = inverse * inverse * inverse * across
        gain = gain_ref[...].reshape(1, width)
        normed = (primal * inverse * gain).astype(BF16)
        dual = (gain * (tangent * inverse - primal * pull)).astype(BF16)
        for block in range(4):
            normed_ref[block, rows, :] = normed[:, block * BLK : (block + 1) * BLK]
            dual_ref[block, rows, :] = dual[:, block * BLK : (block + 1) * BLK]


def kernel(
    q_in,
    dq_in,
    k_in,
    dk_in,
    v_in,
    dv_in,
    q_gain,
    k_gain,
    w_in,
    out,
    dual_out,
    w_all,
    qn,
    dqn,
    kn,
    dkn,
    q_all,
    dq_all,
    k_all,
    dk_all,
    v_all,
    dv_all,
    attn,
    acc,
    give,
    got,
    w_recv,
    w_send,
    first_sem,
    far_recv,
    far_send,
    kv_recv,
    kv_send,
    q_recv,
    q_send,
    own_sem,
    part_recv,
    part_send,
):
    dp = lax.axis_index("dp")
    seq = lax.axis_index("seq")
    z, y, hi = dp // 8, lax.rem(dp // 2, 4), lax.rem(dp, 2)
    lo, core = seq // 2, lax.rem(seq, 2)
    way = 1 - 2 * core

    def unit(zz, yy, hh):
        return zz * 8 + yy * 2 + hh

    def z_at(off):
        return lax.rem(z + off * way + NZ, NZ)

    def y_at(off):
        return lax.rem(y + off * way + NY, NY)

    side = {
        "zf": (unit(z_at(1), y, hi), seq),
        "zb": (unit(z_at(-1), y, hi), seq),
        "yf": (unit(z, y_at(1), hi), seq),
        "yb": (unit(z, y_at(-1), hi), seq),
        "hi": (unit(z, y, 1 - hi), (1 - lo) * 2 + core),
        "lo": (dp, (1 - lo) * 2 + core),
        "cross": (dp, (1 - lo) * 2 + 1 - core),
        "mate": (dp, lo * 2 + 1 - core),
    }

    barrier = pltpu.get_barrier_semaphore()
    for target in side.values():
        pl.semaphore_signal(barrier, inc=1, device_id=target, device_id_type=MESH)
    pl.semaphore_wait(barrier, len(side))

    def remote(src, dst, send_sem, recv_sem, to):
        return pltpu.make_async_remote_copy(
            src_ref=src,
            dst_ref=dst,
            send_sem=send_sem,
            recv_sem=recv_sem,
            device_id=side[to],
            device_id_type=MESH,
        )

    own_w = pltpu.make_async_copy(w_in, w_all.at[lo, dp], first_sem.at[0])
    lo_w = remote(w_in, w_all.at[lo, dp], first_sem.at[1], first_sem.at[2], "lo")

    def piece(stream, source, flip):
        if stream == 0:
            return w_all.at[:, source, pl.ds(0, 32), :]
        block = lo if (stream == 1) != flip else 1 - lo
        return w_all.at[block, source, pl.ds(32, 48), :]

    def w_copy(stream, source, flip, to):
        where = piece(stream, source, flip)
        return remote(where, where, w_send.at[stream], w_recv.at[stream, source], to)

    def own_part(from_input, to):
        block = lo if from_input else 1 - lo
        held = w_in if from_input else w_all.at[block, dp]
        for rows, stream in ((pl.ds(0, 32), 0), (pl.ds(32, 48), 1 if from_input else 2)):
            remote(
                held.at[rows, :],
                w_all.at[block, dp, rows, :],
                w_send.at[stream],
                w_recv.at[stream, dp],
                to,
            ).start()

    lo_w.start()
    for to in ("hi", "yf", "yb", "zf", "zb"):
        own_part(True, to)
    own_w.start()

    def second():
        own_w.wait()
        lo_w.wait_recv()
        for to in ("hi", "yf", "yb", "zf", "zb"):
            own_part(False, to)

    def src(zo, yo, flip):
        return unit(z_at(-zo), y_at(-yo), 1 - hi if flip else hi)

    def z_next(zo):
        if zo == 0:
            return ("zf", "zb")
        if zo > 0:
            return ("zf",) if zo < 4 else ()
        return ("zb",) if zo > -3 else ()

    y_next = {0: ("yf", "yb"), 1: ("yf",), -1: (), 2: ()}

    def w_targets(stream, zo, yo, flip):
        if stream == 0:
            if flip:
                return ()
            return (z_next(zo) if yo == 0 else ()) + y_next[yo] + ("hi",)
        if stream == 1:
            return (y_next[yo] if zo == 0 else ()) + z_next(zo)
        return (z_next(zo) if yo == 0 else ()) + y_next[yo]

    def arrive(stream, zo, yo, flip):
        source = src(zo, yo, flip)
        w_copy(stream, source, flip, "zf").wait_recv()
        for to in w_targets(stream, zo, yo, flip):
            w_copy(stream, source, flip, to).start()

    def mine(group):
        return core + 2 * group

    def theirs(group):
        return 1 - core + 2 * group

    kv_home = (k_all, dk_all, v_all, dv_all)
    whole = pl.ds(0, BLK)

    def kv_source(tensor, block, cols):
        if tensor < 2:
            return (kn, dkn)[tensor].at[block, :, cols]
        first = pl.multiple_of(block * BLK + cols.start, 128)
        return (v_in if tensor == 2 else dv_in).at[:, pl.ds(first, cols.size)]

    def kv_far(head, tensor, which):
        group, cols = head // 5, pl.ds(head % 5 * HDIM, HDIM)
        return remote(
            kv_source(tensor, theirs(group) if which else mine(group), cols),
            kv_home[tensor].at[group, pl.ds((2 + which) * ROWS, ROWS), cols],
            far_send.at[which],
            far_recv.at[head, which],
            ("lo", "cross")[which],
        )

    def kv_mate(group, tensor):
        return remote(
            kv_source(tensor, theirs(group), whole),
            kv_home[tensor].at[group, pl.ds(ROWS, ROWS), :],
            kv_send.at[group, tensor],
            kv_recv.at[group, tensor],
            "mate",
        )

    def kv_own(group, tensor):
        return pltpu.make_async_copy(
            kv_source(tensor, mine(group), whole),
            kv_home[tensor].at[group, pl.ds(0, ROWS), :],
            own_sem.at[group, tensor],
        )

    q_from, q_home = (qn, dqn), (q_all, dq_all)

    def q_copy(group, tensor):
        return remote(
            q_from[tensor].at[theirs(group)],
            q_home[tensor].at[group, pl.ds(ROWS, ROWS), :],
            q_send.at[group, tensor],
            q_recv.at[group, tensor],
            "mate",
        )

    def q_own(group, tensor):
        return pltpu.make_async_copy(
            q_from[tensor].at[mine(group)],
            q_home[tensor].at[group, pl.ds(0, ROWS), :],
            own_sem.at[group, 4 + tensor],
        )

    def send_far(head):
        for tensor in (2, 3, 0, 1):
            for which in range(2):
                kv_far(head, tensor, which).start()

    def start_keys():
        for head in range(4):
            send_far(head)
        for group in range(2):
            for tensor in range(4):
                kv_mate(group, tensor).start()
                kv_own(group, tensor).start()

    def start_queries():
        for group in range(2):
            for tensor in range(2):
                q_copy(group, tensor).start()
                q_own(group, tensor).start()

    def wait_group(group):
        for tensor in range(4):
            kv_own(group, tensor).wait()
            kv_mate(group, tensor).wait_recv()
        for tensor in range(2):
            q_own(group, tensor).wait()
            q_copy(group, tensor).wait_recv()

    factor = HDIM ** (-0.5)
    nt = (((1,), (1,)), ((), ()))

    def head(number):
        if number + 4 < 10:
            send_far(number + 4)
        group, cols = number // 5, pl.ds(number % 5 * HDIM, HDIM)
        if number % 5 == 0:
            wait_group(group)
        for which in range(2):
            four = k_all.at[group, :, cols]
            pltpu.make_async_copy(four, four, far_recv.at[number, which]).wait()
        queries, dual_queries = q_all[group, :, cols], dq_all[group, :, cols]
        keys, dual_keys = k_all[group, :, cols], dk_all[group, :, cols]
        values, dual_values = v_all[group, :, cols], dv_all[group, :, cols]
        scores = lax.dot_general(queries, keys, nt, preferred_element_type=F32) * factor
        dual_scores = (
            lax.dot_general(
                jnp.concatenate([dual_queries, queries], axis=1),
                jnp.concatenate([keys, dual_keys], axis=1),
                nt,
                preferred_element_type=F32,
            )
            * factor
        )
        raised = jnp.exp(scores - jnp.max(scores, axis=-1, keepdims=True))
        probs = raised * (1.0 / jnp.sum(raised, axis=-1, keepdims=True))
        spread = probs * (dual_scores - jnp.sum(probs * dual_scores, axis=-1, keepdims=True))
        low = probs.astype(BF16)
        both = jnp.dot(
            low, jnp.concatenate([values, dual_values], axis=1), preferred_element_type=F32
        )
        dual = both[:, HDIM:] + jnp.dot(spread.astype(BF16), values, preferred_element_type=F32)
        plain = both[:, :HDIM].astype(BF16)
        dual = dual.astype(BF16)
        for owner in range(2):
            rows = slice(owner * ROWS, (owner + 1) * ROWS)
            attn[group, pl.ds(owner * 256, ROWS), cols] = plain[rows]
            attn[group, pl.ds(owner * 256 + ROWS, ROWS), cols] = dual[rows]

    def plane_of(index):
        return z_at(-Z_OFFS[index])

    def product(group, plane, low=0, high=BLK):
        first = pl.multiple_of(plane * 8, 8)
        cols = pl.ds(low, high - low)
        weight = w_all[group, pl.ds(first, 8), :, cols].reshape(PLANE, high - low)
        return lax.dot_general(attn[group, :, cols], weight, nt, preferred_element_type=F32)

    def part_copy(plane, index):
        return remote(
            give.at[index], got.at[plane], part_send.at[index], part_recv.at[plane], "mate"
        )

    def hand_over(index, total):
        acc[index, pl.ds(0, 256), :] = total[:256]
        give[index] = total[256:].astype(BF16)
        part_copy(plane_of(index), index).start()

    def project(kind, index):
        plane = plane_of(index)
        if kind == FIRST:
            acc[index] = product(0, plane)
        elif kind == MIDDLE:
            acc[index] += product(1, plane, 0, 384)
        elif kind == LAST:
            hand_over(index, acc[index] + product(1, plane, 384, BLK))
        elif kind == REST:
            hand_over(index, acc[index] + product(1, plane))
        else:
            hand_over(index, product(0, plane) + product(1, plane))

    def finish(index):
        plane = plane_of(index)
        part_copy(plane, index).wait_recv()
        total = (acc[index, pl.ds(0, 256), :] + got[plane].astype(F32)).astype(BF16)
        cols = pl.ds(pl.multiple_of(plane * PLANE, 128), PLANE)
        out[:, cols] = total[:ROWS]
        dual_out[:, cols] = total[ROWS:]

    for item in ORDER:
        if item < SECOND:
            stream, rest = divmod(item, 64)
            zo, rest = divmod(rest, 8)
            yo, flip = divmod(rest, 2)
            arrive(stream, Z_OFFS[zo], Y_OFFS[yo], flip == 1)
        elif item == SECOND:
            second()
        elif item == KEY_NORM:
            rms_tangent(k_in, dk_in, k_gain, kn, dkn)
        elif item == KEYS:
            start_keys()
        elif item == QUERY_NORM:
            rms_tangent(q_in, dq_in, q_gain, qn, dqn)
        elif item == QUERIES:
            start_queries()
        elif item < FIRST:
            head(item - HEAD)
        elif item < FINISH:
            project(item // 10 * 10, item % 10)
        else:
            finish(item - FINISH)

    lo_w.wait_send()
    for which in range(2):
        pltpu.make_async_copy(k_all, k_all, far_send.at[which]).wait()
    for group in range(2):
        for tensor in range(4):
            kv_mate(group, tensor).wait_send()
        for tensor in range(2):
            q_copy(group, tensor).wait_send()
    sent = (w_all.at[:, pl.ds(0, 63), pl.ds(0, 32), :],) + tuple(
        w_all.at[j, pl.ds(0, 63), pl.ds(32, 48), :] for j in range(2)
    )
    for stream in range(3):
        pltpu.make_async_copy(sent[stream], sent[stream], w_send.at[stream]).wait()
    for index in range(8):
        part_copy(plane_of(index), index).wait_send()


def body(q, k, v, dq, dk, dv, q_gain, k_gain, weight):
    rows, width = q.shape
    vmem = pl.BlockSpec(memory_space=pltpu.VMEM)
    hbm = pl.BlockSpec(memory_space=pl.ANY)
    sem = pltpu.SemaphoreType.DMA
    kv = pltpu.VMEM((2, 4 * ROWS, BLK), BF16)
    qs = pltpu.VMEM((2, 2 * ROWS, BLK), BF16)
    normed = pltpu.VMEM((4, ROWS, BLK), BF16)
    shape = jax.ShapeDtypeStruct((rows, 2 * width), BF16)
    return pl.pallas_call(
        kernel,
        out_shape=(shape, shape),
        in_specs=[vmem] * 4 + [hbm] * 2 + [vmem] * 2 + [hbm],
        out_specs=(vmem, vmem),
        scratch_shapes=[
            pltpu.VMEM((2, 64, UNIT, BLK), BF16),
            normed,
            normed,
            normed,
            normed,
            qs,
            qs,
            kv,
            kv,
            kv,
            kv,
            pltpu.VMEM((2, 4 * ROWS, BLK), BF16),
            pltpu.VMEM((8, 4 * ROWS, PLANE), F32),
            pltpu.VMEM((8, 2 * ROWS, PLANE), BF16),
            pltpu.VMEM((8, 2 * ROWS, PLANE), BF16),
            sem((3, 64)),
            sem((3,)),
            sem((3,)),
            sem((10, 2)),
            sem((2,)),
            sem((2, 4)),
            sem((2, 4)),
            sem((2, 2)),
            sem((2, 2)),
            sem((2, 6)),
            sem((8,)),
            sem((8,)),
        ],
        compiler_params=pltpu.CompilerParams(
            collective_id=0, has_side_effects=True, vmem_limit_bytes=60 * 1024 * 1024
        ),
        name="tangent_attention",
    )(q, dq, k, dk, v, dv, q_gain, k_gain, weight.T)


def solution(mesh):
    tokens = P(("dp", "seq"), None)
    return jax.shard_map(
        body,
        mesh=mesh,
        in_specs=(tokens,) * 6 + (P(), P(), P("seq", "dp")),
        out_specs=(tokens, tokens),
        check_vma=False,
    )
```

time: 126 us -> 94.5 us (0.75); the launches traced: 124 us -> 94.4 us
  Pallas kernels: 117 us -> 90.1 us
  local copies, waits for them, and re-layouts: 6.25 us -> 3.62 us
    pallas_call x1, Pallas kernels: 117 us -> 90.1 us  [body(): pl.pallas_call(kernel, out_shape=(shape, shape), in_specs=[vmem] * 4 + [h...]
    reshape x2 -> x0, local copies, waits for them, and re-layouts: 2.63 us -> none  [the longest x1 1.31 us: body(): q_gain.reshape(1, width)]
where the time goes in v2:
time: 94.5 us; the launch traced here: 94.4 us
  Pallas kernels  90.1 us (95%)
  local copies, waits for them, and re-layouts  3.62 us (4%)
    pallas_call x1, Pallas kernels, body(): pl.pallas_call(kernel, out_shape=(shape, shape), in_specs=[vmem] * 4 + [h...  90.1 us
    unnamed x4, local copies, waits for them, and re-layouts  3.62 us

profile of v2, /device:TPU:1, one launch (start us, length us, event | category | flops | bytes accessed | tf_op | source)
XLA Modules:
  0.0 94.4 jit_solution(15906433767731331539)
XLA Ops:
  0.6 90.1 %tangent_attention.1 = (bf16[128,5120]{1,0:T(8,128)(2,1)}, bf16[128,5120]{1,0:T(8,128)(2,1)}) custom-call(bf16[128,2560]{1,0:T(8,128)(2,1)} %q_in.1, bf16[128,2560]{1,0:T(8,128)(2,1)} %dq_in.1, bf16[128,2560]{1,0:T(8,128)(2,1)} %k_in.1, bf16[128,2560]{1,0:T(8,128)(2,1)} %dk_in.1, bf16[128,2560]{1,0:T(8,128)(2,1)} %v_in.1, bf16[128,2560]{1,0:T(8,128)(2,1)} %dv_in.1, ...), custom_call_target="tpu_custom_call" | custom-call | tf_op jit(solution)/shard_map/tangent_attention/pallas_call | solution.py:415
  90.7 0.0 copy-start
  90.8 2.6 %copy.13 = bf16[128,5120]{1,0:T(8,128)(2,1)} copy(bf16[128,5120]{1,0:T(8,128)(2,1)} %get-tuple-element.4) | data formatting | bytes 2621440
  93.3 0.0 copy-done
  93.3 1.1 %copy.14 = bf16[128,5120]{1,0:T(8,128)(2,1)} copy(bf16[128,5120]{1,0:T(8,128)(2,1)S(1)} %copy-done) | data formatting | bytes 2621440
Async XLA Ops:
  90.7 2.6 %copy-start = (bf16[128,5120]{1,0:T(8,128)(2,1)S(1)}, bf16[128,5120]{1,0:T(8,128)(2,1)}, u32[]{:S(2)}) copy-start(bf16[128,5120]{1,0:T(8,128)(2,1)} %get-tuple-element.5) | copy-start | bytes 3932164

commit v3 on v2

--- a/solution.py
+++ b/solution.py
@@ -18,21 +18,29 @@
 
 Z_OFFS = (0, 1, -1, 2, -2, 3, -3, 4)
 Y_OFFS = (0, 1, -1, 2)
-SECOND, KEY_NORM, KEYS, QUERY_NORM, QUERIES, HEAD = 200, 201, 202, 203, 204, 300
-FIRST, MIDDLE, LAST, REST, WHOLE, FINISH = 400, 410, 420, 430, 440, 450
+SECOND, KEY_NORM, KEYS, QUERY_NORM, QUERIES, HEAD = 400, 401, 402, 403, 404, 500
+FIRST, MIDDLE, LAST, REST, WHOLE = 600, 610, 620, 630, 640
+STREAMS = (
+    (0, 32, True, "zyh"),
+    (0, 32, False, "zyh"),
+    (32, 48, True, "hyz"),
+    (32, 48, False, "hzy"),
+)
 ORDER = (
-    201, 202, 72, 80, 66, 68, 65, 200, 203, 204, 88, 70, 96, 69, 1, 4, 74, 67, 82, 129, 2, 132, 76,
-    84, 130, 73, 81, 71, 300, 5, 8, 16, 133, 131, 6, 136, 144, 3, 134, 104, 86, 78, 112, 10, 12, 9,
-    301, 77, 85, 18, 20, 17, 90, 83, 135, 140, 7, 75, 98, 138, 148, 137, 145, 146, 11, 14, 92, 302,
-    100, 22, 13, 89, 97, 141, 142, 19, 79, 87, 149, 139, 147, 21, 24, 32, 150, 303, 152, 143, 160,
-    15, 151, 120, 102, 23, 28, 26, 94, 101, 25, 93, 36, 99, 34, 106, 156, 114, 304, 33, 154, 91,
-    164, 161, 162, 400, 29, 30, 153, 116, 401, 38, 27, 108, 113, 402, 158, 165, 105, 103, 37, 305,
-    163, 157, 95, 166, 48, 35, 155, 40, 176, 31, 168, 118, 167, 39, 110, 404, 117, 52, 50, 306, 109,
-    115, 49, 44, 159, 122, 177, 403, 180, 41, 107, 119, 42, 172, 169, 53, 178, 124, 181, 121, 307,
-    170, 111, 51, 56, 410, 173, 54, 184, 179, 411, 45, 126, 46, 412, 125, 413, 123, 171, 43, 185,
-    414, 60, 127, 182, 308, 57, 188, 174, 55, 189, 58, 186, 183, 406, 47, 175, 405, 187, 61, 309,
-    62, 190, 420, 59, 421, 191, 422, 423, 450, 424, 451, 452, 63, 435, 453, 454, 436, 447, 455, 456,
-    457,
+    401, 402, 8, 16, 2, 4, 1, 400, 136, 144, 130, 132, 129, 403, 404, 24, 10, 12, 32, 9, 18, 20, 72,
+    80, 17, 6, 68, 3, 200, 208, 66, 196, 5, 500, 152, 160, 194, 133, 65, 138, 146, 134, 28, 193, 36,
+    25, 140, 148, 131, 76, 11, 26, 137, 145, 84, 13, 14, 40, 48, 33, 34, 204, 501, 88, 96, 22, 19,
+    212, 21, 216, 224, 74, 73, 82, 197, 168, 176, 81, 44, 202, 7, 141, 149, 52, 69, 210, 92, 154,
+    162, 67, 502, 70, 100, 29, 142, 150, 198, 220, 37, 201, 209, 77, 195, 228, 27, 135, 156, 164,
+    30, 85, 42, 50, 139, 147, 15, 503, 38, 41, 153, 161, 90, 205, 49, 56, 112, 98, 35, 213, 104,
+    218, 240, 89, 226, 232, 78, 97, 165, 86, 23, 184, 60, 504, 206, 116, 178, 75, 157, 83, 214, 166,
+    108, 45, 170, 203, 225, 53, 244, 158, 93, 211, 151, 236, 71, 199, 600, 217, 46, 180, 101, 505,
+    54, 143, 31, 163, 94, 229, 43, 58, 172, 114, 177, 51, 102, 155, 39, 106, 181, 221, 91, 222, 169,
+    182, 242, 57, 120, 506, 230, 241, 234, 113, 248, 99, 207, 167, 105, 227, 173, 79, 601, 124, 215,
+    179, 186, 87, 602, 174, 219, 61, 245, 233, 62, 507, 118, 159, 117, 183, 252, 109, 610, 110, 188,
+    611, 246, 47, 171, 612, 122, 55, 185, 189, 243, 95, 237, 190, 238, 59, 249, 250, 115, 175, 231,
+    508, 103, 187, 223, 603, 613, 235, 126, 107, 604, 121, 614, 247, 125, 253, 191, 251, 63, 254,
+    119, 606, 239, 616, 111, 509, 620, 123, 621, 255, 127, 622, 623, 624, 645, 626, 647,
 )
 
 
@@ -65,6 +73,8 @@
     w_in,
     out,
     dual_out,
+    got,
+    dual_got,
     w_all,
     qn,
     dqn,
@@ -79,7 +89,7 @@
     attn,
     acc,
     give,
-    got,
+    keep,
     w_recv,
     w_send,
     first_sem,
@@ -92,6 +102,7 @@
     own_sem,
     part_recv,
     part_send,
+    out_sem,
 ):
     dp = lax.axis_index("dp")
     seq = lax.axis_index("seq")
@@ -138,26 +149,21 @@
     lo_w = remote(w_in, w_all.at[lo, dp], first_sem.at[1], first_sem.at[2], "lo")
 
     def piece(stream, source, flip):
-        if stream == 0:
-            return w_all.at[:, source, pl.ds(0, 32), :]
-        block = lo if (stream == 1) != flip else 1 - lo
-        return w_all.at[block, source, pl.ds(32, 48), :]
+        first, count, began, _ = STREAMS[stream]
+        block = lo if began != flip else 1 - lo
+        return w_all.at[block, source, pl.ds(first, count), :]
 
     def w_copy(stream, source, flip, to):
         where = piece(stream, source, flip)
         return remote(where, where, w_send.at[stream], w_recv.at[stream, source], to)
 
-    def own_part(from_input, to):
-        block = lo if from_input else 1 - lo
-        held = w_in if from_input else w_all.at[block, dp]
-        for rows, stream in ((pl.ds(0, 32), 0), (pl.ds(32, 48), 1 if from_input else 2)):
-            remote(
-                held.at[rows, :],
-                w_all.at[block, dp, rows, :],
-                w_send.at[stream],
-                w_recv.at[stream, dp],
-                to,
-            ).start()
+    def own_part(began, to):
+        for stream, (first, count, from_input, _) in enumerate(STREAMS):
+            if from_input != began:
+                continue
+            where = piece(stream, dp, False)
+            held = w_in.at[pl.ds(first, count), :] if began else where
+            remote(held, where, w_send.at[stream], w_recv.at[stream, dp], to).start()
 
     lo_w.start()
     for to in ("hi", "yf", "yb", "zf", "zb"):
@@ -183,11 +189,12 @@
     y_next = {0: ("yf", "yb"), 1: ("yf",), -1: (), 2: ()}
 
     def w_targets(stream, zo, yo, flip):
-        if stream == 0:
+        axes = STREAMS[stream][3]
+        if axes == "zyh":
             if flip:
                 return ()
             return (z_next(zo) if yo == 0 else ()) + y_next[yo] + ("hi",)
-        if stream == 1:
+        if axes == "hyz":
             return (y_next[yo] if zo == 0 else ()) + z_next(zo)
         return (z_next(zo) if yo == 0 else ()) + y_next[yo]
 
@@ -332,15 +339,33 @@
         weight = w_all[group, pl.ds(first, 8), :, cols].reshape(PLANE, high - low)
         return lax.dot_general(attn[group, :, cols], weight, nt, preferred_element_type=F32)
 
-    def part_copy(plane, index):
-        return remote(
-            give.at[index], got.at[plane], part_send.at[index], part_recv.at[plane], "mate"
-        )
+    def out_copies(index):
+        first = pl.multiple_of(plane_of(index) * PLANE, 128)
+        cols = pl.ds(first, PLANE)
+        copies = []
+        for half in range(2):
+            rows = pl.ds(half * ROWS, ROWS)
+            copies.append(
+                remote(
+                    give.at[index, rows, :],
+                    (got, dual_got)[half].at[:, cols],
+                    part_send.at[index, half],
+                    part_recv.at[plane_of(index), half],
+                    "mate",
+                )
+            )
+            copies.append(
+                pltpu.make_async_copy(
+                    keep.at[index, rows, :], (out, dual_out)[half].at[:, cols], out_sem.at[index, half]
+                )
+            )
+        return copies
 
     def hand_over(index, total):
-        acc[index, pl.ds(0, 256), :] = total[:256]
         give[index] = total[256:].astype(BF16)
-        part_copy(plane_of(index), index).start()
+        keep[index] = total[:256].astype(BF16)
+        for copy in out_copies(index):
+            copy.start()
 
     def project(kind, index):
         plane = plane_of(index)
@@ -354,14 +379,6 @@
             hand_over(index, acc[index] + product(1, plane))
         else:
             hand_over(index, product(0, plane) + product(1, plane))
-
-    def finish(index):
-        plane = plane_of(index)
-        part_copy(plane, index).wait_recv()
-        total = (acc[index, pl.ds(0, 256), :] + got[plane].astype(F32)).astype(BF16)
-        cols = pl.ds(pl.multiple_of(plane * PLANE, 128), PLANE)
-        out[:, cols] = total[:ROWS]
-        dual_out[:, cols] = total[ROWS:]
 
     for item in ORDER:
         if item < SECOND:
@@ -381,10 +398,8 @@
             start_queries()
         elif item < FIRST:
             head(item - HEAD)
-        elif item < FINISH:
+        else:
             project(item // 10 * 10, item % 10)
-        else:
-            finish(item - FINISH)
 
     lo_w.wait_send()
     for which in range(2):
@@ -394,13 +409,12 @@
             kv_mate(group, tensor).wait_send()
         for tensor in range(2):
             q_copy(group, tensor).wait_send()
-    sent = (w_all.at[:, pl.ds(0, 63), pl.ds(0, 32), :],) + tuple(
-        w_all.at[j, pl.ds(0, 63), pl.ds(32, 48), :] for j in range(2)
-    )
-    for stream in range(3):
-        pltpu.make_async_copy(sent[stream], sent[stream], w_send.at[stream]).wait()
+    for stream, (first, count, _, _) in enumerate(STREAMS):
+        sent = w_all.at[0, pl.ds(0, 63), pl.ds(first, count), :]
+        pltpu.make_async_copy(sent, sent, w_send.at[stream]).wait()
     for index in range(8):
-        part_copy(plane_of(index), index).wait_send()
+        for copy in out_copies(index):
+            copy.wait()
 
 
 def body(q, k, v, dq, dk, dv, q_gain, k_gain, weight):
@@ -412,11 +426,11 @@
     qs = pltpu.VMEM((2, 2 * ROWS, BLK), BF16)
     normed = pltpu.VMEM((4, ROWS, BLK), BF16)
     shape = jax.ShapeDtypeStruct((rows, 2 * width), BF16)
-    return pl.pallas_call(
+    plain, dual, got, dual_got = pl.pallas_call(
         kernel,
-        out_shape=(shape, shape),
+        out_shape=(shape,) * 4,
         in_specs=[vmem] * 4 + [hbm] * 2 + [vmem] * 2 + [hbm],
-        out_specs=(vmem, vmem),
+        out_specs=(hbm,) * 4,
         scratch_shapes=[
             pltpu.VMEM((2, 64, UNIT, BLK), BF16),
             normed,
@@ -433,8 +447,8 @@
             pltpu.VMEM((8, 4 * ROWS, PLANE), F32),
             pltpu.VMEM((8, 2 * ROWS, PLANE), BF16),
             pltpu.VMEM((8, 2 * ROWS, PLANE), BF16),
-            sem((3, 64)),
-            sem((3,)),
+            sem((4, 64)),
+            sem((4,)),
             sem((3,)),
             sem((10, 2)),
             sem((2,)),
@@ -443,14 +457,19 @@
             sem((2, 2)),
             sem((2, 2)),
             sem((2, 6)),
-            sem((8,)),
-            sem((8,)),
+            sem((8, 2)),
+            sem((8, 2)),
+            sem((8, 2)),
         ],
         compiler_params=pltpu.CompilerParams(
             collective_id=0, has_side_effects=True, vmem_limit_bytes=60 * 1024 * 1024
         ),
         name="tangent_attention",
     )(q, dq, k, dk, v, dv, q_gain, k_gain, weight.T)
+    return (
+        (plain.astype(F32) + got.astype(F32)).astype(BF16),
+        (dual.astype(F32) + dual_got.astype(F32)).astype(BF16),
+    )
 
 
 def solution(mesh):

time: 94.5 us -> 90.3 us (0.956)
  Pallas kernels: 90.1 us -> 84.6 us
  other arithmetic: 0 us -> 4.96 us
  local copies, waits for them, and re-layouts: 3.62 us -> 0 us
    pallas_call x1, Pallas kernels: 90.1 us -> 84.6 us  [body(): pl.pallas_call(kernel, out_shape=(shape,) * 4, in_specs=[vmem] * 4 + [hbm...]
    convert_element_type x0 -> x1, other arithmetic: none -> 4.96 us  [body(): (dual.astype(F32) + dual_got.astype(F32)).astype(BF16)]
    unnamed x4 -> x0, local copies, waits for them, and re-layouts: 3.62 us -> none
where the time goes in v3:
time: 90.3 us; the launch traced here: 90.2 us
  Pallas kernels  84.6 us (94%)
  other arithmetic  4.96 us (5%)
    pallas_call x1, Pallas kernels, body(): pl.pallas_call(kernel, out_shape=(shape,) * 4, in_specs=[vmem] * 4 + [hbm...  84.6 us
    convert_element_type x1, other arithmetic, body(): (dual.astype(F32) + dual_got.astype(F32)).astype(BF16)  4.96 us

profile of v3, /device:TPU:1, one launch (start us, length us, event | category | flops | bytes accessed | tf_op | source)
XLA Modules:
  0.0 90.2 jit_solution(9068043610961904757)
XLA Ops:
  0.6 84.6 %tangent_attention.1 = (bf16[128,5120]{1,0:T(8,128)(2,1)}, bf16[128,5120]{1,0:T(8,128)(2,1)}, bf16[128,5120]{1,0:T(8,128)(2,1)}, bf16[128,5120]{1,0:T(8,128)(2,1)}) custom-call(bf16[128,2560]{1,0:T(8,128)(2,1)} %q_in.1, bf16[128,2560]{1,0:T(8,128)(2,1)} %dq_in.1, bf16[128,2560]{1,0:T(8,128)(2,1)} %k_in.1, bf16[128,2560]{1,0:T(8,128)(2,1)} %dk_in.1, ...), custom_call_target="tpu_custom_call" | custom-call | tf_op jit(solution)/shard_map/tangent_attention/pallas_call | solution.py:429
  85.2 5.0 %add_convert_fusion = (bf16[128,5120]{1,0:T(8,128)(2,1)}, bf16[128,5120]{1,0:T(8,128)(2,1)}) fusion(bf16[128,5120]{1,0:T(8,128)(2,1)} %get-tuple-element.9, bf16[128,5120]{1,0:T(8,128)(2,1)} %get-tuple-element.8, bf16[128,5120]{1,0:T(8,128)(2,1)} %get-tuple-element.7, bf16[128,5120]{1,0:T(8,128)(2,1)} %get-tuple-element.6), kind=kLoop, calls=%fused_computation | loop fusion | flops 5242880 | bytes 7864320 | tf_op jit(solution)/shard_map/convert_element_type | solution.py:471

commit v4 on v3

--- a/solution.py
+++ b/solution.py
@@ -75,6 +75,12 @@
     dual_out,
     got,
     dual_got,
+    q_raw,
+    dq_raw,
+    k_raw,
+    dk_raw,
+    q_scale,
+    k_scale,
     w_all,
     qn,
     dqn,
@@ -90,6 +96,7 @@
     acc,
     give,
     keep,
+    load_sem,
     w_recv,
     w_send,
     first_sem,
@@ -104,6 +111,21 @@
     part_send,
     out_sem,
 ):
+    def load(which):
+        source, home = loads[which]
+        return pltpu.make_async_copy(source, home, load_sem.at[which])
+
+    loads = (
+        (k_in, k_raw),
+        (dk_in, dk_raw),
+        (k_gain, k_scale),
+        (q_in, q_raw),
+        (dq_in, dq_raw),
+        (q_gain, q_scale),
+    )
+    for which in range(6):
+        load(which).start()
+
     dp = lax.axis_index("dp")
     seq = lax.axis_index("seq")
     z, y, hi = dp // 8, lax.rem(dp // 2, 4), lax.rem(dp, 2)
@@ -389,11 +411,15 @@
         elif item == SECOND:
             second()
         elif item == KEY_NORM:
-            rms_tangent(k_in, dk_in, k_gain, kn, dkn)
+            for which in range(3):
+                load(which).wait()
+            rms_tangent(k_raw, dk_raw, k_scale, kn, dkn)
         elif item == KEYS:
             start_keys()
         elif item == QUERY_NORM:
-            rms_tangent(q_in, dq_in, q_gain, qn, dqn)
+            for which in range(3, 6):
+                load(which).wait()
+            rms_tangent(q_raw, dq_raw, q_scale, qn, dqn)
         elif item == QUERIES:
             start_queries()
         elif item < FIRST:
@@ -419,19 +445,27 @@
 
 def body(q, k, v, dq, dk, dv, q_gain, k_gain, weight):
     rows, width = q.shape
-    vmem = pl.BlockSpec(memory_space=pltpu.VMEM)
-    hbm = pl.BlockSpec(memory_space=pl.ANY)
+    hbm = pl.BlockSpec(memory_space=pltpu.HBM)
+    free = pl.BlockSpec(memory_space=pl.ANY)
     sem = pltpu.SemaphoreType.DMA
     kv = pltpu.VMEM((2, 4 * ROWS, BLK), BF16)
     qs = pltpu.VMEM((2, 2 * ROWS, BLK), BF16)
     normed = pltpu.VMEM((4, ROWS, BLK), BF16)
+    raw = pltpu.VMEM((rows, width), BF16)
+    scale = pltpu.VMEM((width,), F32)
     shape = jax.ShapeDtypeStruct((rows, 2 * width), BF16)
     plain, dual, got, dual_got = pl.pallas_call(
         kernel,
         out_shape=(shape,) * 4,
-        in_specs=[vmem] * 4 + [hbm] * 2 + [vmem] * 2 + [hbm],
-        out_specs=(hbm,) * 4,
+        in_specs=[hbm] * 9,
+        out_specs=(free,) * 4,
         scratch_shapes=[
+            raw,
+            raw,
+            raw,
+            raw,
+            scale,
+            scale,
             pltpu.VMEM((2, 64, UNIT, BLK), BF16),
             normed,
             normed,
@@ -447,6 +481,7 @@
             pltpu.VMEM((8, 4 * ROWS, PLANE), F32),
             pltpu.VMEM((8, 2 * ROWS, PLANE), BF16),
             pltpu.VMEM((8, 2 * ROWS, PLANE), BF16),
+            sem((6,)),
             sem((4, 64)),
             sem((4,)),
             sem((3,)),
@@ -462,10 +497,10 @@
             sem((8, 2)),
         ],
         compiler_params=pltpu.CompilerParams(
-            collective_id=0, has_side_effects=True, vmem_limit_bytes=60 * 1024 * 1024
+            collective_id=0, has_side_effects=True, vmem_limit_bytes=44 * 1024 * 1024
         ),
         name="tangent_attention",
-    )(q, dq, k, dk, v, dv, q_gain, k_gain, weight.T)
+    )(*(pltpu.with_memory_space_constraint(a, pltpu.HBM) for a in (q, dq, k, dk, v, dv, q_gain, k_gain, weight.T)))
     return (
         (plain.astype(F32) + got.astype(F32)).astype(BF16),
         (dual.astype(F32) + dual_got.astype(F32)).astype(BF16),

time: 90.3 us -> 86.4 us (0.957)
  other arithmetic: 4.96 us -> 2.46 us
  Pallas kernels: 84.6 us -> 83.2 us
    convert_element_type x1, other arithmetic: 4.96 us -> 2.46 us  [body(): (dual.astype(F32) + dual_got.astype(F32)).astype(BF16)]
    pallas_call x1, Pallas kernels: 84.6 us -> 83.2 us  [body(): pl.pallas_call(kernel, out_shape=(shape,) * 4, in_specs=[hbm] * 9, out_sp...]
where the time goes in v4:
time: 86.4 us; the launch traced here: 86.3 us
  Pallas kernels  83.2 us (96%)
  other arithmetic  2.46 us (3%)
    pallas_call x1, Pallas kernels, body(): pl.pallas_call(kernel, out_shape=(shape,) * 4, in_specs=[hbm] * 9, out_sp...  83.2 us
    convert_element_type x1, other arithmetic, body(): (dual.astype(F32) + dual_got.astype(F32)).astype(BF16)  2.46 us

profile of v4, /device:TPU:1, one launch (start us, length us, event | category | flops | bytes accessed | tf_op | source)
XLA Modules:
  0.0 86.3 jit_solution(4740986918600667059)
XLA Ops:
  0.6 83.2 %tangent_attention.1 = (bf16[128,5120]{1,0:T(8,128)(2,1)S(1)}, bf16[128,5120]{1,0:T(8,128)(2,1)S(1)}, bf16[128,5120]{1,0:T(8,128)(2,1)S(1)}, bf16[128,5120]{1,0:T(8,128)(2,1)S(1)}) custom-call(bf16[128,2560]{1,0:T(8,128)(2,1)} %q_in.1, bf16[128,2560]{1,0:T(8,128)(2,1)} %dq_in.1, bf16[128,2560]{1,0:T(8,128)(2,1)} %k_in.1, bf16[128,2560]{1,0:T(8,128)(2,1)} %dk_in.1, ...), custom_call_target="tpu_custom_call" | custom-call | tf_op jit(solution)/shard_map/tangent_attention/pallas_call | solution.py:457
  83.9 2.5 %add_convert_fusion = (bf16[128,5120]{1,0:T(8,128)(2,1)}, bf16[128,5120]{1,0:T(8,128)(2,1)}) fusion(bf16[128,5120]{1,0:T(8,128)(2,1)S(1)} %get-tuple-element.9, bf16[128,5120]{1,0:T(8,128)(2,1)S(1)} %get-tuple-element.8, bf16[128,5120]{1,0:T(8,128)(2,1)S(1)} %get-tuple-element.7, bf16[128,5120]{1,0:T(8,128)(2,1)S(1)} %get-tuple-element.6), kind=kLoop, calls=%fused_computation | loop fusion | flops 5242880 | bytes 7864320 | tf_op jit(solution)/shard_map/convert_element_type | solution.py:506

commit v5 on v4

--- a/solution.py
+++ b/solution.py
@@ -20,27 +20,46 @@
 Y_OFFS = (0, 1, -1, 2)
 SECOND, KEY_NORM, KEYS, QUERY_NORM, QUERIES, HEAD = 400, 401, 402, 403, 404, 500
 FIRST, MIDDLE, LAST, REST, WHOLE = 600, 610, 620, 630, 640
+SEND = 1000
+SIDES = ("hi", "yf", "yb", "zf", "zb")
 STREAMS = (
-    (0, 32, True, "zyh"),
-    (0, 32, False, "zyh"),
-    (32, 48, True, "hyz"),
-    (32, 48, False, "hzy"),
+    (True, ((0, 32, 0, 512),)),
+    (False, ((0, 32, 0, 640),)),
+    (True, ((32, 48, 0, 640), (0, 32, 512, 128))),
+    (False, ((32, 48, 0, 640),)),
 )
+PARTS = tuple((stream, part) for stream, (_, parts) in enumerate(STREAMS) for part in parts)
 ORDER = (
-    401, 402, 8, 16, 2, 4, 1, 400, 136, 144, 130, 132, 129, 403, 404, 24, 10, 12, 32, 9, 18, 20, 72,
-    80, 17, 6, 68, 3, 200, 208, 66, 196, 5, 500, 152, 160, 194, 133, 65, 138, 146, 134, 28, 193, 36,
-    25, 140, 148, 131, 76, 11, 26, 137, 145, 84, 13, 14, 40, 48, 33, 34, 204, 501, 88, 96, 22, 19,
-    212, 21, 216, 224, 74, 73, 82, 197, 168, 176, 81, 44, 202, 7, 141, 149, 52, 69, 210, 92, 154,
-    162, 67, 502, 70, 100, 29, 142, 150, 198, 220, 37, 201, 209, 77, 195, 228, 27, 135, 156, 164,
-    30, 85, 42, 50, 139, 147, 15, 503, 38, 41, 153, 161, 90, 205, 49, 56, 112, 98, 35, 213, 104,
-    218, 240, 89, 226, 232, 78, 97, 165, 86, 23, 184, 60, 504, 206, 116, 178, 75, 157, 83, 214, 166,
-    108, 45, 170, 203, 225, 53, 244, 158, 93, 211, 151, 236, 71, 199, 600, 217, 46, 180, 101, 505,
-    54, 143, 31, 163, 94, 229, 43, 58, 172, 114, 177, 51, 102, 155, 39, 106, 181, 221, 91, 222, 169,
-    182, 242, 57, 120, 506, 230, 241, 234, 113, 248, 99, 207, 167, 105, 227, 173, 79, 601, 124, 215,
-    179, 186, 87, 602, 174, 219, 61, 245, 233, 62, 507, 118, 159, 117, 183, 252, 109, 610, 110, 188,
-    611, 246, 47, 171, 612, 122, 55, 185, 189, 243, 95, 237, 190, 238, 59, 249, 250, 115, 175, 231,
-    508, 103, 187, 223, 603, 613, 235, 126, 107, 604, 121, 614, 247, 125, 253, 191, 251, 63, 254,
-    119, 606, 239, 616, 111, 509, 620, 123, 621, 255, 127, 622, 623, 624, 645, 626, 647,
+    1003, 1004, 1641, 1642, 1640, 1643, 1644, 1001, 1002, 1000, 401, 402, 8, 1043, 16, 1084, 1041,
+    1042, 1040, 1081, 1082, 1080, 130, 1653, 132, 1654, 1663, 1664, 1651, 129, 136, 400, 144, 2, 4,
+    1647, 1960, 1646, 1322, 1320, 1323, 1324, 1321, 1962, 1010, 403, 1963, 1964, 1961, 1020, 404,
+    24, 1122, 32, 10, 1123, 12, 1164, 1120, 1162, 1121, 18, 20, 1648, 1160, 1649, 1161, 138, 146,
+    1050, 134, 1673, 1060, 1674, 133, 1011, 193, 1967, 1968, 140, 1090, 1969, 148, 68, 1051, 131,
+    1100, 72, 1362, 500, 80, 66, 1402, 1363, 1404, 1656, 1340, 1361, 1360, 200, 2002, 208, 28, 2042,
+    1401, 194, 1400, 40, 2003, 48, 36, 2044, 1202, 26, 1330, 1201, 34, 1668, 137, 1669, 1242, 145,
+    1140, 6, 1241, 1658, 76, 1659, 1200, 14, 1091, 142, 150, 84, 1240, 1203, 501, 135, 201, 2007,
+    1966, 1679, 209, 2047, 1331, 1180, 1130, 74, 2008, 2001, 88, 2049, 1442, 96, 1170, 1482, 82,
+    1030, 1441, 216, 1443, 44, 42, 224, 1484, 2082, 1380, 1481, 1678, 52, 50, 1070, 2122, 22, 141,
+    149, 2124, 1420, 2041, 2083, 502, 195, 139, 147, 1370, 1683, 1724, 1131, 1440, 70, 56, 1282,
+    1281, 1734, 92, 1480, 1693, 151, 202, 217, 2087, 1171, 100, 1744, 1410, 2088, 2006, 90, 104,
+    225, 1522, 2127, 1220, 1521, 2129, 98, 112, 1562, 1210, 1561, 1523, 143, 1260, 210, 240, 2202,
+    1729, 503, 60, 232, 30, 1703, 2046, 2162, 1250, 1110, 1371, 58, 160, 1754, 1350, 1688, 38, 152,
+    1411, 1280, 108, 1713, 1749, 162, 1460, 203, 2081, 154, 1500, 106, 1708, 1739, 1211, 164, 116,
+    1450, 233, 2167, 2121, 114, 1520, 120, 241, 1602, 1698, 1759, 2207, 504, 211, 1601, 1490, 1251,
+    156, 1718, 161, 78, 1804, 1560, 86, 2086, 1300, 153, 2163, 166, 1814, 1451, 218, 2126, 1150, 46,
+    1491, 124, 1290, 158, 2168, 165, 1824, 2201, 1190, 2161, 226, 505, 157, 122, 163, 54, 1291,
+    1540, 1763, 1809, 1531, 1530, 219, 2166, 1580, 1773, 155, 94, 167, 1834, 1571, 2206, 1570, 227,
+    1783, 102, 1611, 1600, 159, 1829, 1971, 242, 1390, 1976, 234, 1768, 248, 2242, 2241, 62, 1819,
+    1430, 110, 506, 249, 235, 118, 2247, 1793, 1839, 2246, 1230, 1620, 2011, 243, 168, 1788, 126,
+    1610, 2051, 1270, 2016, 170, 1778, 1470, 2056, 2091, 1510, 172, 1798, 2131, 1310, 250, 507, 251,
+    169, 1843, 2096, 1550, 2136, 1853, 1590, 2211, 1863, 1, 65, 3, 196, 5, 197, 69, 67, 7, 71, 198,
+    199, 174, 2171, 1630, 600, 1848, 610, 173, 1873, 2176, 2216, 171, 1868, 2251, 175, 1858, 2256,
+    508, 1878, 9, 11, 13, 204, 73, 205, 77, 15, 75, 79, 206, 207, 601, 611, 17, 19, 21, 212, 81,
+    213, 85, 83, 23, 87, 214, 215, 602, 612, 25, 29, 27, 220, 89, 221, 93, 91, 31, 222, 95, 223,
+    603, 613, 33, 37, 35, 228, 97, 229, 101, 99, 39, 230, 103, 231, 604, 614, 509, 620, 621, 622,
+    623, 624, 41, 45, 43, 236, 237, 105, 109, 107, 47, 111, 238, 239, 645, 49, 53, 51, 244, 245,
+    113, 176, 178, 180, 117, 177, 115, 182, 181, 179, 183, 55, 246, 119, 247, 646, 57, 61, 59, 252,
+    121, 253, 125, 123, 63, 184, 186, 188, 185, 127, 190, 254, 189, 255, 187, 191, 647,
 )
 
 
@@ -170,61 +189,33 @@
     own_w = pltpu.make_async_copy(w_in, w_all.at[lo, dp], first_sem.at[0])
     lo_w = remote(w_in, w_all.at[lo, dp], first_sem.at[1], first_sem.at[2], "lo")
 
-    def piece(stream, source, flip):
-        first, count, began, _ = STREAMS[stream]
-        block = lo if began != flip else 1 - lo
-        return w_all.at[block, source, pl.ds(first, count), :]
-
-    def w_copy(stream, source, flip, to):
-        where = piece(stream, source, flip)
-        return remote(where, where, w_send.at[stream], w_recv.at[stream, source], to)
-
-    def own_part(began, to):
-        for stream, (first, count, from_input, _) in enumerate(STREAMS):
-            if from_input != began:
+    def src(zo, yo, flip):
+        return unit(z_at(-zo), y_at(-yo), 1 - hi if flip else hi)
+
+    def w_copies(code, to):
+        stream, rest = divmod(code, 64)
+        zo, rest = divmod(rest, 8)
+        yo, flip = divmod(rest, 2)
+        source = src(Z_OFFS[zo], Y_OFFS[yo], flip)
+        began = STREAMS[stream][0]
+        block = lo if began != (flip == 1) else 1 - lo
+        copies = []
+        for index, (owner, (row, rows, col, cols)) in enumerate(PARTS):
+            if owner != stream:
                 continue
-            where = piece(stream, dp, False)
-            held = w_in.at[pl.ds(first, count), :] if began else where
-            remote(held, where, w_send.at[stream], w_recv.at[stream, dp], to).start()
+            where = w_all.at[block, source, pl.ds(row, rows), pl.ds(col, cols)]
+            held = where
+            if began and rest == 0 and zo == 0:
+                held = w_in.at[pl.ds(row, rows), pl.ds(col, cols)]
+            copies.append(remote(held, where, w_send.at[index], w_recv.at[index, source], to))
+        return copies
 
     lo_w.start()
-    for to in ("hi", "yf", "yb", "zf", "zb"):
-        own_part(True, to)
     own_w.start()
 
     def second():
         own_w.wait()
         lo_w.wait_recv()
-        for to in ("hi", "yf", "yb", "zf", "zb"):
-            own_part(False, to)
-
-    def src(zo, yo, flip):
-        return unit(z_at(-zo), y_at(-yo), 1 - hi if flip else hi)
-
-    def z_next(zo):
-        if zo == 0:
-            return ("zf", "zb")
-        if zo > 0:
-            return ("zf",) if zo < 4 else ()
-        return ("zb",) if zo > -3 else ()
-
-    y_next = {0: ("yf", "yb"), 1: ("yf",), -1: (), 2: ()}
-
-    def w_targets(stream, zo, yo, flip):
-        axes = STREAMS[stream][3]
-        if axes == "zyh":
-            if flip:
-                return ()
-            return (z_next(zo) if yo == 0 else ()) + y_next[yo] + ("hi",)
-        if axes == "hyz":
-            return (y_next[yo] if zo == 0 else ()) + z_next(zo)
-        return (z_next(zo) if yo == 0 else ()) + y_next[yo]
-
-    def arrive(stream, zo, yo, flip):
-        source = src(zo, yo, flip)
-        w_copy(stream, source, flip, "zf").wait_recv()
-        for to in w_targets(stream, zo, yo, flip):
-            w_copy(stream, source, flip, to).start()
 
     def mine(group):
         return core + 2 * group
@@ -403,11 +394,13 @@
             hand_over(index, product(0, plane) + product(1, plane))
 
     for item in ORDER:
-        if item < SECOND:
-            stream, rest = divmod(item, 64)
-            zo, rest = divmod(rest, 8)
-            yo, flip = divmod(rest, 2)
-            arrive(stream, Z_OFFS[zo], Y_OFFS[yo], flip == 1)
+        if item >= SEND:
+            code, way_out = divmod(item - SEND, 5)
+            for copy in w_copies(code, SIDES[way_out]):
+                copy.start()
+        elif item < SECOND:
+            for copy in w_copies(item, "zf"):
+                copy.wait_recv()
         elif item == SECOND:
             second()
         elif item == KEY_NORM:
@@ -435,9 +428,9 @@
             kv_mate(group, tensor).wait_send()
         for tensor in range(2):
             q_copy(group, tensor).wait_send()
-    for stream, (first, count, _, _) in enumerate(STREAMS):
-        sent = w_all.at[0, pl.ds(0, 63), pl.ds(first, count), :]
-        pltpu.make_async_copy(sent, sent, w_send.at[stream]).wait()
+    for index, (_, (row, rows, col, cols)) in enumerate(PARTS):
+        sent = w_all.at[0, pl.ds(0, 63), pl.ds(row, rows), pl.ds(col, cols)]
+        pltpu.make_async_copy(sent, sent, w_send.at[index]).wait()
     for index in range(8):
         for copy in out_copies(index):
             copy.wait()
@@ -482,8 +475,8 @@
             pltpu.VMEM((8, 2 * ROWS, PLANE), BF16),
             pltpu.VMEM((8, 2 * ROWS, PLANE), BF16),
             sem((6,)),
-            sem((4, 64)),
-            sem((4,)),
+            sem((5, 64)),
+            sem((5,)),
             sem((3,)),
             sem((10, 2)),
             sem((2,)),

time: 86.4 us -> 84.5 us (0.978)
  Pallas kernels: 83.2 us -> 81.3 us
    pallas_call x1, Pallas kernels: 83.2 us -> 81.3 us  [body(): pl.pallas_call(kernel, out_shape=(shape,) * 4, in_specs=[hbm] * 9, out_sp...]
where the time goes in v5:
time: 84.5 us; the launch traced here: 84.4 us
  Pallas kernels  81.3 us (96%)
  other arithmetic  2.46 us (3%)
    pallas_call x1, Pallas kernels, body(): pl.pallas_call(kernel, out_shape=(shape,) * 4, in_specs=[hbm] * 9, out_sp...  81.3 us
    convert_element_type x1, other arithmetic, body(): (dual.astype(F32) + dual_got.astype(F32)).astype(BF16)  2.46 us

profile of v5, /device:TPU:1, one launch (start us, length us, event | category | flops | bytes accessed | tf_op | source)
XLA Modules:
  0.0 84.4 jit_solution(2107482417504571145)
XLA Ops:
  0.6 81.3 %tangent_attention.1 = (bf16[128,5120]{1,0:T(8,128)(2,1)S(1)}, bf16[128,5120]{1,0:T(8,128)(2,1)S(1)}, bf16[128,5120]{1,0:T(8,128)(2,1)S(1)}, bf16[128,5120]{1,0:T(8,128)(2,1)S(1)}) custom-call(bf16[128,2560]{1,0:T(8,128)(2,1)} %q_in.1, bf16[128,2560]{1,0:T(8,128)(2,1)} %dq_in.1, bf16[128,2560]{1,0:T(8,128)(2,1)} %k_in.1, bf16[128,2560]{1,0:T(8,128)(2,1)} %dk_in.1, ...), custom_call_target="tpu_custom_call" | custom-call | tf_op jit(solution)/shard_map/tangent_attention/pallas_call | solution.py:450
  82.0 2.5 %add_convert_fusion = (bf16[128,5120]{1,0:T(8,128)(2,1)}, bf16[128,5120]{1,0:T(8,128)(2,1)}) fusion(bf16[128,5120]{1,0:T(8,128)(2,1)S(1)} %get-tuple-element.9, bf16[128,5120]{1,0:T(8,128)(2,1)S(1)} %get-tuple-element.8, bf16[128,5120]{1,0:T(8,128)(2,1)S(1)} %get-tuple-element.7, bf16[128,5120]{1,0:T(8,128)(2,1)S(1)} %get-tuple-element.6), kind=kLoop, calls=%fused_computation | loop fusion | flops 5242880 | bytes 7864320 | tf_op jit(solution)/shard_map/convert_element_type | solution.py:499

commit v6 on v5

--- a/solution.py
+++ b/solution.py
@@ -434,6 +434,23 @@
     for index in range(8):
         for copy in out_copies(index):
             copy.wait()
+
+
+def add_sums(plain, dual, got, dual_got, out, dual_out, total, sems):
+    def copy(half, part):
+        rows = pl.ds(part * 16, 16)
+        return pltpu.make_async_copy(
+            total.at[half, rows, :], (out, dual_out)[half].at[rows, :], sems.at[half, part]
+        )
+
+    for part in range(8):
+        rows = pl.ds(part * 16, 16)
+        for half, (mine, theirs) in enumerate(((plain, got), (dual, dual_got))):
+            total[half, rows, :] = (mine[rows, :].astype(F32) + theirs[rows, :].astype(F32)).astype(BF16)
+            copy(half, part).start()
+    for part in range(8):
+        for half in range(2):
+            copy(half, part).wait()
 
 
 def body(q, k, v, dq, dk, dv, q_gain, k_gain, weight):
@@ -494,10 +511,16 @@
         ),
         name="tangent_attention",
     )(*(pltpu.with_memory_space_constraint(a, pltpu.HBM) for a in (q, dq, k, dk, v, dv, q_gain, k_gain, weight.T)))
-    return (
-        (plain.astype(F32) + got.astype(F32)).astype(BF16),
-        (dual.astype(F32) + dual_got.astype(F32)).astype(BF16),
-    )
+    vmem = pl.BlockSpec(memory_space=pltpu.VMEM)
+    return pl.pallas_call(
+        add_sums,
+        out_shape=(shape, shape),
+        in_specs=[vmem] * 4,
+        out_specs=(hbm, hbm),
+        scratch_shapes=[pltpu.VMEM((2, rows, 2 * width), BF16), sem((2, 8))],
+        compiler_params=pltpu.CompilerParams(vmem_limit_bytes=16 * 1024 * 1024),
+        name="add_sums",
+    )(plain, dual, got, dual_got)
 
 
 def solution(mesh):

time: 84.5 us -> 83.9 us (level)
  other arithmetic: 2.46 us -> 0 us
  Pallas kernels: 81.3 us -> 83 us
    convert_element_type x1 -> x0, other arithmetic: 2.46 us -> none  [body(): (dual.astype(F32) + dual_got.astype(F32)).astype(BF16)]
    pallas_call x0 -> x1, Pallas kernels: none -> 1.66 us  [body(): pl.pallas_call(add_sums, out_shape=(shape, shape), in_specs=[vmem] * 4, o...]
where the time goes in v6:
time: 83.9 us; the launch traced here: 83.8 us
  Pallas kernels  83 us (99%)
    pallas_call x1, Pallas kernels, body(): pl.pallas_call(kernel, out_shape=(shape,) * 4, in_specs=[hbm] * 9, out_sp...  81.3 us

profile of v6, /device:TPU:1, one launch (start us, length us, event | category | flops | bytes accessed | tf_op | source)
XLA Modules:
  0.0 83.8 jit_solution(13063020222398646034)
XLA Ops:
  0.6 81.3 %tangent_attention.1 = (bf16[128,5120]{1,0:T(8,128)(2,1)S(1)}, bf16[128,5120]{1,0:T(8,128)(2,1)S(1)}, bf16[128,5120]{1,0:T(8,128)(2,1)S(1)}, bf16[128,5120]{1,0:T(8,128)(2,1)S(1)}) custom-call(bf16[128,2560]{1,0:T(8,128)(2,1)} %q_in.1, bf16[128,2560]{1,0:T(8,128)(2,1)} %dq_in.1, bf16[128,2560]{1,0:T(8,128)(2,1)} %k_in.1, bf16[128,2560]{1,0:T(8,128)(2,1)} %dk_in.1, ...), custom_call_target="tpu_custom_call" | custom-call | tf_op jit(solution)/shard_map/tangent_attention/pallas_call | solution.py:467
  82.0 1.7 %add_sums.1 = (bf16[128,5120]{1,0:T(8,128)(2,1)}, bf16[128,5120]{1,0:T(8,128)(2,1)}) custom-call(bf16[128,5120]{1,0:T(8,128)(2,1)S(1)} %get-tuple-element.6.plain, bf16[128,5120]{1,0:T(8,128)(2,1)S(1)} %get-tuple-element.7.dual, bf16[128,5120]{1,0:T(8,128)(2,1)S(1)} %get-tuple-element.8.got, bf16[128,5120]{1,0:T(8,128)(2,1)S(1)} %get-tuple-element.9.dual_got), custom_call_target="tpu_custom_call" | custom-call | tf_op jit(solution)/shard_map/add_sums/pallas_call | solution.py:515
